TPU v7x, 512 devices: a whole 4x4x16 slice. The times are simulated.
512 devices in a mesh: ta: 16 (over z), gz: 4 (over x), gy: 8 (over y, core).
Axes of the slice: x: 4, y: 4, z: 16, core: 2. Of those that a mesh axis runs over, the one named last changes fastest.
Arguments:
- state: float32 [16, 8, 16, 64, 128], P('ta', None, 'gz', 'gy'), may hold values from -6 to 6
- step_index: int32 [16], P('ta'), may hold values from 0 to 999
- sched_index: int32 [16], P('ta'), may hold values from 0 to 999
- coef_table: float32 [1000, 2], replicated, may hold values from 0.1 to 0.6
- time_weight: float32 [64, 64], replicated, may hold values from -0.75 to 0.75
- w_in: bfloat16 [3, 3, 3, 8, 64], replicated, may hold values from -0.4375 to 0.4375
- w_mid1: bfloat16 [3, 3, 3, 64, 64], replicated, may hold values from -0.15625 to 0.15625
- w_mid2: bfloat16 [3, 3, 3, 64, 64], replicated, may hold values from -0.15625 to 0.15625
- w_out: bfloat16 [3, 3, 3, 64, 8], replicated, may hold values from -0.15625 to 0.15625
Outputs:
- new_state: float32 [16, 8, 16, 64, 128], P('ta', None, 'gz', 'gy')
All inputs are finite; a program needn't handle non-finite values.
Results may differ from a plain program's by a relative error of at most 0.0013.
Values may be sent and summed in bfloat16 or wider, within the bound.
No kernel may reach another device: no remote copies, remote signals or barrier semaphores. Data moves between devices by JAX's collectives and lax.ppermute only.
A program may use at most 64 MiB of HBM per device.

v0:
```python
import jax
import jax.numpy as jnp
from jax import lax
from jax.sharding import PartitionSpec as P


def with_halo(value, sides, width):
    for axis, dim in sides:
        size, length = (lax.axis_size(axis), value.shape[dim])
        up = [(i, (i + 1) % size) for i in range(size - 1)]
        down = [(j, i) for i, j in up]
        last = lax.slice_in_dim(value, length - width, length, axis=dim)
        leading = lax.slice_in_dim(value, 0, width, axis=dim)
        before = lax.ppermute(last, axis, up)
        after = lax.ppermute(leading, axis, down)
        value = jnp.concatenate([before, value, after], axis=dim)
    return value


def entering(part, axis, combine, identity):
    place = lax.axis_index(axis)
    gathered = lax.all_gather(part, axis)
    state = jnp.zeros_like(part) + jnp.asarray(identity, part.dtype)

    def one(step, state):
        return combine(state, lax.dynamic_index_in_dim(gathered, step, 0, False))

    return lax.fori_loop(0, place, one, state)


def conv_valid(padded, kernel):
    framed = jnp.pad(padded, ((0, 0), (0, 0), (0, 0), (1, 1)))
    out_z = padded.shape[1] - 2
    out_y = padded.shape[2] - 2
    width = padded.shape[3]
    channels = padded.shape[0]
    stacked = jnp.concatenate(
        [framed[:, :, :, 0:width], framed[:, :, :, 1 : width + 1], framed[:, :, :, 2 : width + 2]],
        axis=0,
    )
    total = jnp.zeros((kernel.shape[4], out_z, out_y, width), jnp.float32)
    for shift_z in range(3):
        for shift_y in range(3):
            window = stacked[:, shift_z : shift_z + out_z, shift_y : shift_y + out_y, :]
            taps = kernel[shift_z, shift_y].reshape(3 * channels, kernel.shape[4])
            total = total + jnp.einsum(
                "czyx,cd->dzyx", window, taps, preferred_element_type=jnp.float32
            )
    return total


def time_features(step, time_weight):
    half = time_weight.shape[0] // 2
    freqs = jnp.exp(-jnp.log(1000.0) * jnp.arange(half, dtype=jnp.float32) / half)
    angles = step.astype(jnp.float32) * freqs
    feats = jnp.concatenate([jnp.sin(angles), jnp.cos(angles)])
    return jnp.dot(feats, time_weight, precision=lax.Precision.HIGHEST)


def add_terms(earlier, later):
    return earlier + later


def on_device(state, step_index, sched_index, coef_table, time_weight, w_in, w_mid1, w_mid2, w_out):
    own = state[0]
    inputs = own.astype(jnp.bfloat16)
    bias = time_features(step_index[0], time_weight)
    kernels = [w_in, w_mid1, w_mid2, w_out]
    hidden = inputs
    for layer in range(4):
        padded = with_halo(hidden, (("gz", 1), ("gy", 2)), 1)
        summed = conv_valid(padded, kernels[layer])
        if layer == 0:
            summed = summed + bias[:, None, None, None]
        if layer < 3:
            hidden = jax.nn.silu(summed).astype(jnp.bfloat16)
        else:
            hidden = summed
    entries = jnp.arange(coef_table.shape[0], dtype=jnp.int32)
    picked = entries == sched_index[0]
    coef_a = jnp.sum(jnp.where(picked, coef_table[:, 0], 0.0))
    coef_b = jnp.sum(jnp.where(picked, coef_table[:, 1], 0.0))
    drift = coef_b * hidden - coef_a * own
    drift = drift + jnp.where(lax.axis_index("ta") == 0, own, jnp.zeros_like(own))
    anchor = jnp.zeros_like(own)
    before = entering(drift, "ta", add_terms, jnp.zeros_like(drift))
    total = before + drift
    return (anchor + total)[None]


def solution(mesh):
    placed = (P("ta", None, "gz", "gy", None), P("ta"), P("ta"), P(), P(), P(), P(), P(), P())
    return jax.shard_map(
        on_device,
        mesh=mesh,
        in_specs=placed,
        out_specs=P("ta", None, "gz", "gy", None),
        check_vma=False,
    )
```

profile of v0, /device:TPU:480, one launch (start us, length us, event | category | flops | bytes accessed | tf_op | source)
XLA Modules:
  0.0 202.7 jit_solution(6147651219253774140)
XLA Ops:
  7.6 3.4 %collective-permute-start = (bf16[8,1,8,128]{3,0,2,1:T(8,128)(2,1)S(1)}, bf16[8,1,8,128]{3,0,2,1:T(8,128)(2,1)S(1)}, u32[]{:S(2)}, u32[]{:S(2)}) collective-permute-start(bf16[8,1,8,128]{3,0,2,1:T(8,128)(2,1)S(1)} %get-tuple-element.85), channel_id=1, source_target_pairs={{0,8},{8,16},{16,24},{1,9},{9,17},{17,25},{2,10},{10,18},{18,26},{... | collective-permute-start | bytes 49160 | tf_op jit(solution)/shard_map/ppermute | solution.py:14
  11.0 1.3 collective-permute-start.1
  13.0 3.6 %collective-permute-done.1 = bf16[8,1,8,128]{3,0,2,1:T(8,128)(2,1)S(1)} collective-permute-done((bf16[8,1,8,128]{3,0,2,1:T(8,128)(2,1)S(1)}, bf16[8,1,8,128]{3,0,2,1:T(8,128)(2,1)S(1)}, u32[]{:S(2)}, u32[]{:S(2)}) %collective-permute-start.1) | collective-permute-done | bytes 16416 | tf_op jit(solution)/shard_map/ppermute | solution.py:15
  16.6 1.3 collective-permute-start.2
  17.9 1.3 collective-permute-start.3
  19.4 3.4 %collective-permute-done.3 = bf16[8,6,1,128]{3,0,2,1:T(8,128)(2,1)S(1)} collective-permute-done((bf16[8,6,1,128]{3,0,2,1:T(8,128)(2,1)S(1)}, bf16[8,6,1,128]{3,0,2,1:T(8,128)(2,1)S(1)}, u32[]{:S(2)}, u32[]{:S(2)}) %collective-permute-start.3) | collective-permute-done | bytes 12320 | tf_op jit(solution)/shard_map/ppermute | solution.py:15
  27.2 3.4 %collective-permute-start.4 = (bf16[64,1,8,128]{3,0,2,1:T(8,128)(2,1)S(1)}, bf16[64,1,8,128]{3,0,2,1:T(8,128)(2,1)S(1)}, u32[]{:S(2)}, u32[]{:S(2)}) collective-permute-start(bf16[64,1,8,128]{3,0,2,1:T(8,128)(2,1)S(1)} %get-tuple-element.61), channel_id=1, source_target_pairs={{0,8},{8,16},{16,24},{1,9},{9,17},{17,25},{2,10},{10,18},{18,26},{... | collective-permute-start | bytes 393224 | tf_op jit(solution)/shard_map/ppermute | solution.py:14
  30.6 1.3 collective-permute-start.5
  31.9 1.2 collective-permute-done.4
  33.1 4.6 %collective-permute-done.5 = bf16[64,1,8,128]{3,0,2,1:T(8,128)(2,1)S(1)} collective-permute-done((bf16[64,1,8,128]{3,0,2,1:T(8,128)(2,1)S(1)}, bf16[64,1,8,128]{3,0,2,1:T(8,128)(2,1)S(1)}, u32[]{:S(2)}, u32[]{:S(2)}) %collective-permute-start.5) | collective-permute-done | bytes 131104 | tf_op jit(solution)/shard_map/ppermute | solution.py:15
  37.7 2.9 %collective-permute-start.6 = (bf16[64,6,1,128]{3,0,2,1:T(8,128)(2,1)S(1)}, bf16[64,6,1,128]{3,0,2,1:T(8,128)(2,1)S(1)}, u32[]{:S(2)}, u32[]{:S(2)}) collective-permute-start(bf16[64,6,1,128]{3,0,2,1:T(8,128)(2,1)S(1)} %get-tuple-element.55), channel_id=1, source_target_pairs={{0,1},{1,2},{2,3},{3,4},{4,5},{5,6},{6,7},{8,9},{9,10},{10,11},{11... | collective-permute-start | bytes 294920 | tf_op jit(solution)/shard_map/ppermute | solution.py:14
  40.6 1.3 collective-permute-start.7
  42.0 3.6 %collective-permute-done.7 = bf16[64,6,1,128]{3,0,2,1:T(8,128)(2,1)S(1)} collective-permute-done((bf16[64,6,1,128]{3,0,2,1:T(8,128)(2,1)S(1)}, bf16[64,6,1,128]{3,0,2,1:T(8,128)(2,1)S(1)}, u32[]{:S(2)}, u32[]{:S(2)}) %collective-permute-start.7) | collective-permute-done | bytes 98336 | tf_op jit(solution)/shard_map/ppermute | solution.py:15
  45.5 1.8 fusion.18
  53.6 3.1 %collective-permute-start.8 = (bf16[64,1,8,128]{3,0,2,1:T(8,128)(2,1)S(1)}, bf16[64,1,8,128]{3,0,2,1:T(8,128)(2,1)S(1)}, u32[]{:S(2)}, u32[]{:S(2)}) collective-permute-start(bf16[64,1,8,128]{3,0,2,1:T(8,128)(2,1)S(1)} %get-tuple-element.59), channel_id=1, source_target_pairs={{0,8},{8,16},{16,24},{1,9},{9,17},{17,25},{2,10},{10,18},{18,26},{... | collective-permute-start | bytes 393224 | tf_op jit(solution)/shard_map/ppermute | solution.py:14
  56.7 1.3 collective-permute-start.9
  59.2 4.4 %collective-permute-done.9 = bf16[64,1,8,128]{3,0,2,1:T(8,128)(2,1)S(1)} collective-permute-done((bf16[64,1,8,128]{3,0,2,1:T(8,128)(2,1)S(1)}, bf16[64,1,8,128]{3,0,2,1:T(8,128)(2,1)S(1)}, u32[]{:S(2)}, u32[]{:S(2)}) %collective-permute-start.9) | collective-permute-done | bytes 131104 | tf_op jit(solution)/shard_map/ppermute | solution.py:15
  63.6 3.7 %collective-permute-start.10 = (bf16[64,6,1,128]{3,0,2,1:T(8,128)(2,1)S(1)}, bf16[64,6,1,128]{3,0,2,1:T(8,128)(2,1)S(1)}, u32[]{:S(2)}, u32[]{:S(2)}) collective-permute-start(bf16[64,6,1,128]{3,0,2,1:T(8,128)(2,1)S(1)} %get-tuple-element.53), channel_id=1, source_target_pairs={{0,1},{1,2},{2,3},{3,4},{4,5},{5,6},{6,7},{8,9},{9,10},{10,11},{11... | collective-permute-start | bytes 294920 | tf_op jit(solution)/shard_map/ppermute | solution.py:14
  67.3 1.5 collective-permute-start.11
  70.3 1.6 collective-permute-done.11
  71.9 1.8 fusion.16
  80.0 1.6 collective-permute-start.12
  81.6 1.3 collective-permute-start.13
  83.0 1.2 collective-permute-done.12
  84.1 4.4 %collective-permute-done.13 = bf16[64,1,8,128]{3,0,2,1:T(8,128)(2,1)S(1)} collective-permute-done((bf16[64,1,8,128]{3,0,2,1:T(8,128)(2,1)S(1)}, bf16[64,1,8,128]{3,0,2,1:T(8,128)(2,1)S(1)}, u32[]{:S(2)}, u32[]{:S(2)}) %collective-permute-start.13) | collective-permute-done | bytes 131104 | tf_op jit(solution)/shard_map/ppermute | solution.py:15
  88.5 3.7 %collective-permute-start.14 = (bf16[64,6,1,128]{3,0,2,1:T(8,128)(2,1)S(1)}, bf16[64,6,1,128]{3,0,2,1:T(8,128)(2,1)S(1)}, u32[]{:S(2)}, u32[]{:S(2)}) collective-permute-start(bf16[64,6,1,128]{3,0,2,1:T(8,128)(2,1)S(1)} %get-tuple-element.51), channel_id=1, source_target_pairs={{0,1},{1,2},{2,3},{3,4},{4,5},{5,6},{6,7},{8,9},{9,10},{10,11},{11... | collective-permute-start | bytes 294920 | tf_op jit(solution)/shard_map/ppermute | solution.py:14
  92.3 1.3 collective-permute-start.15
  94.2 2.3 %collective-permute-done.15 = bf16[64,6,1,128]{3,0,2,1:T(8,128)(2,1)S(1)} collective-permute-done((bf16[64,6,1,128]{3,0,2,1:T(8,128)(2,1)S(1)}, bf16[64,6,1,128]{3,0,2,1:T(8,128)(2,1)S(1)}, u32[]{:S(2)}, u32[]{:S(2)}) %collective-permute-start.15) | collective-permute-done | bytes 98336 | tf_op jit(solution)/shard_map/ppermute | solution.py:15
  96.6 1.8 select_maximum_fusion
  102.6 2.3 %fusion.53 = f32[8,4,8,128]{3,0,2,1:T(8,128)} fusion(f32[4,8,128,8]{2,3,1,0:T(8,128)S(1)} %fusion.81, f32[4,8,128,8]{2,3,1,0:T(8,128)S(1)} %fusion.83, f32[4,8,128,8]{2,3,1,0:T(8,128)S(1)} %fusion.85, f32[4,8,128,8]{2,3,1,0:T(8,128)S(1)} %fusion.87, f32[4,8,128,8]{2,3,1,0:T(8,128)S(1)} %fusion.89, f32[4,8,128,8]{2,3,1,0:T(8,128)S(1)} %fusion.91, ...), kind=kOutput, calls=%fused_computation.73 | convolution fusion | flops 13008896 | bytes 4262921 | tf_op jit(solution)/shard_map/czyx,cd->dzyx/dot_general | solution.py:46
  104.9 75.1 %all-gather.3.cloned.1.call-done = f32[128,4,8,128]{3,0,2,1:T(8,128)} async-done(((f32[8,4,8,128]{3,0,2,1:T(8,128)}), f32[128,4,8,128]{3,0,2,1:T(8,128)}) %all-gather.3.cloned.1.call-update) | async-done | bytes 2097168 | tf_op jit(solution)/shard_map/all_gather | solution.py:22
  180.1 15.0 %while.10 = (s32[]{:T(128)}, f32[8,4,8,128]{3,2,1,0:T(8,128)S(1)}, s32[]{:T(128)}, f32[16,8,4,8,128]{4,1,0,3,2:T(8,128)}, s32[]{:T(128)}, /*index=5*/s32[]{:T(128)}, s32[]{:T(128)}) while((s32[]{:T(128)}, f32[8,4,8,128]{3,2,1,0:T(8,128)S(1)}, s32[]{:T(128)}, f32[16,8,4,8,128]{4,1,0,3,2:T(8,128)}, s32[]{:T(128)}, /*index=5*/s32[]{:T(128)}, ...), condition=%wide.region_3.4_spmd, body=%wide.region_2.3_spmd.sunk | while | flops 32773 | bytes 655475 | solution.py:28
  (134 shorter events, 40.2 us)
Async XLA Ops:
  6.5 12.7 %copy-start = (f32[64,64]{1,0:T(8,128)S(1)}, f32[64,64]{1,0:T(8,128)}, u32[]{:S(2)}) copy-start(f32[64,64]{1,0:T(8,128)} %param.15) | copy-start | bytes 49156
  6.5 17.6 %copy-start.6 = (bf16[3,3,3,8,64]{4,3,2,1,0:T(8,128)(2,1)S(1)}, bf16[3,3,3,8,64]{4,3,2,1,0:T(8,128)(2,1)}, u32[]{:S(2)}) copy-start(bf16[3,3,3,8,64]{4,3,2,1,0:T(8,128)(2,1)} %param.16) | copy-start | bytes 82948
  6.5 173.5 %all-gather.3.cloned.1.call-start = ((), (), s32[]{:S(2)}) async-start(), calls=%async_computation | async-start | bytes 2228224 | tf_op jit(solution)/shard_map/all_gather | solution.py:22
  7.6 5.4 %collective-permute-start = (bf16[8,1,8,128]{3,0,2,1:T(8,128)(2,1)S(1)}, bf16[8,1,8,128]{3,0,2,1:T(8,128)(2,1)S(1)}, u32[]{:S(2)}, u32[]{:S(2)}) collective-permute-start(bf16[8,1,8,128]{3,0,2,1:T(8,128)(2,1)S(1)} %get-tuple-element.85), channel_id=1, source_target_pairs={{0,8},{8,16},{16,24},{1,9},{9,17},{17,25},{2,10},{10,18},{18,26},{... | collective-permute-start | bytes 49160 | tf_op jit(solution)/shard_map/ppermute | solution.py:14
  11.0 5.6 %collective-permute-start.1 = (bf16[8,1,8,128]{3,0,2,1:T(8,128)(2,1)S(1)}, bf16[8,1,8,128]{3,0,2,1:T(8,128)(2,1)S(1)}, u32[]{:S(2)}, u32[]{:S(2)}) collective-permute-start(bf16[8,1,8,128]{3,0,2,1:T(8,128)(2,1)S(1)} %get-tuple-element.86), channel_id=1, source_target_pairs={{8,0},{16,8},{24,16},{9,1},{17,9},{25,17},{10,2},{18,10},{26,18},{... | collective-permute-start | bytes 49160 | tf_op jit(solution)/shard_map/ppermute | solution.py:15
  16.6 2.8 %collective-permute-start.2 = (bf16[8,6,1,128]{3,0,2,1:T(8,128)(2,1)S(1)}, bf16[8,6,1,128]{3,0,2,1:T(8,128)(2,1)S(1)}, u32[]{:S(2)}, u32[]{:S(2)}) collective-permute-start(bf16[8,6,1,128]{3,0,2,1:T(8,128)(2,1)S(1)} %get-tuple-element.83), channel_id=1, source_target_pairs={{0,1},{1,2},{2,3},{3,4},{4,5},{5,6},{6,7},{8,9},{9,10},{10,11},{11... | collective-permute-start | bytes 36872 | tf_op jit(solution)/shard_map/ppermute | solution.py:14
  17.9 4.9 %collective-permute-start.3 = (bf16[8,6,1,128]{3,0,2,1:T(8,128)(2,1)S(1)}, bf16[8,6,1,128]{3,0,2,1:T(8,128)(2,1)S(1)}, u32[]{:S(2)}, u32[]{:S(2)}) collective-permute-start(bf16[8,6,1,128]{3,0,2,1:T(8,128)(2,1)S(1)} %get-tuple-element.84), channel_id=1, source_target_pairs={{1,0},{2,1},{3,2},{4,3},{5,4},{6,5},{7,6},{9,8},{10,9},{11,10},{12... | collective-permute-start | bytes 36872 | tf_op jit(solution)/shard_map/ppermute | solution.py:15
  26.6 15.3 %copy-start.3 = (bf16[3,3,3,64,64]{4,3,2,1,0:T(8,128)(2,1)S(1)}, bf16[3,3,3,64,64]{4,3,2,1,0:T(8,128)(2,1)}, u32[]{:S(2)}) copy-start(bf16[3,3,3,64,64]{4,3,2,1,0:T(8,128)(2,1)} %param.17) | copy-start | bytes 663556
  27.2 5.9 %collective-permute-start.4 = (bf16[64,1,8,128]{3,0,2,1:T(8,128)(2,1)S(1)}, bf16[64,1,8,128]{3,0,2,1:T(8,128)(2,1)S(1)}, u32[]{:S(2)}, u32[]{:S(2)}) collective-permute-start(bf16[64,1,8,128]{3,0,2,1:T(8,128)(2,1)S(1)} %get-tuple-element.61), channel_id=1, source_target_pairs={{0,8},{8,16},{16,24},{1,9},{9,17},{17,25},{2,10},{10,18},{18,26},{... | collective-permute-start | bytes 393224 | tf_op jit(solution)/shard_map/ppermute | solution.py:14
  30.6 7.1 %collective-permute-start.5 = (bf16[64,1,8,128]{3,0,2,1:T(8,128)(2,1)S(1)}, bf16[64,1,8,128]{3,0,2,1:T(8,128)(2,1)S(1)}, u32[]{:S(2)}, u32[]{:S(2)}) collective-permute-start(bf16[64,1,8,128]{3,0,2,1:T(8,128)(2,1)S(1)} %get-tuple-element.62), channel_id=1, source_target_pairs={{8,0},{16,8},{24,16},{9,1},{17,9},{25,17},{10,2},{18,10},{26,18},{... | collective-permute-start | bytes 393224 | tf_op jit(solution)/shard_map/ppermute | solution.py:15
  37.7 4.3 %collective-permute-start.6 = (bf16[64,6,1,128]{3,0,2,1:T(8,128)(2,1)S(1)}, bf16[64,6,1,128]{3,0,2,1:T(8,128)(2,1)S(1)}, u32[]{:S(2)}, u32[]{:S(2)}) collective-permute-start(bf16[64,6,1,128]{3,0,2,1:T(8,128)(2,1)S(1)} %get-tuple-element.55), channel_id=1, source_target_pairs={{0,1},{1,2},{2,3},{3,4},{4,5},{5,6},{6,7},{8,9},{9,10},{10,11},{11... | collective-permute-start | bytes 294920 | tf_op jit(solution)/shard_map/ppermute | solution.py:14
  40.6 4.9 %collective-permute-start.7 = (bf16[64,6,1,128]{3,0,2,1:T(8,128)(2,1)S(1)}, bf16[64,6,1,128]{3,0,2,1:T(8,128)(2,1)S(1)}, u32[]{:S(2)}, u32[]{:S(2)}) collective-permute-start(bf16[64,6,1,128]{3,0,2,1:T(8,128)(2,1)S(1)} %get-tuple-element.56), channel_id=1, source_target_pairs={{1,0},{2,1},{3,2},{4,3},{5,4},{6,5},{7,6},{9,8},{10,9},{11,10},{12... | collective-permute-start | bytes 294920 | tf_op jit(solution)/shard_map/ppermute | solution.py:15
  52.6 5.4 %copy-start.4 = (bf16[3,3,3,64,64]{4,3,2,1,0:T(8,128)(2,1)S(1)}, bf16[3,3,3,64,64]{4,3,2,1,0:T(8,128)(2,1)}, u32[]{:S(2)}) copy-start(bf16[3,3,3,64,64]{4,3,2,1,0:T(8,128)(2,1)} %param.18) | copy-start | bytes 663556
  52.7 16.1 %copy-start.5 = (bf16[3,3,3,64,8]{3,4,2,1,0:T(8,128)(2,1)S(1)}, bf16[3,3,3,64,8]{3,4,2,1,0:T(8,128)(2,1)}, u32[]{:S(2)}) copy-start(bf16[3,3,3,64,8]{3,4,2,1,0:T(8,128)(2,1)} %param.19) | copy-start | bytes 82948
  53.6 5.6 %collective-permute-start.8 = (bf16[64,1,8,128]{3,0,2,1:T(8,128)(2,1)S(1)}, bf16[64,1,8,128]{3,0,2,1:T(8,128)(2,1)S(1)}, u32[]{:S(2)}, u32[]{:S(2)}) collective-permute-start(bf16[64,1,8,128]{3,0,2,1:T(8,128)(2,1)S(1)} %get-tuple-element.59), channel_id=1, source_target_pairs={{0,8},{8,16},{16,24},{1,9},{9,17},{17,25},{2,10},{10,18},{18,26},{... | collective-permute-start | bytes 393224 | tf_op jit(solution)/shard_map/ppermute | solution.py:14
  56.7 6.9 %collective-permute-start.9 = (bf16[64,1,8,128]{3,0,2,1:T(8,128)(2,1)S(1)}, bf16[64,1,8,128]{3,0,2,1:T(8,128)(2,1)S(1)}, u32[]{:S(2)}, u32[]{:S(2)}) collective-permute-start(bf16[64,1,8,128]{3,0,2,1:T(8,128)(2,1)S(1)} %get-tuple-element.60), channel_id=1, source_target_pairs={{8,0},{16,8},{24,16},{9,1},{17,9},{25,17},{10,2},{18,10},{26,18},{... | collective-permute-start | bytes 393224 | tf_op jit(solution)/shard_map/ppermute | solution.py:15
  63.6 6.7 %collective-permute-start.10 = (bf16[64,6,1,128]{3,0,2,1:T(8,128)(2,1)S(1)}, bf16[64,6,1,128]{3,0,2,1:T(8,128)(2,1)S(1)}, u32[]{:S(2)}, u32[]{:S(2)}) collective-permute-start(bf16[64,6,1,128]{3,0,2,1:T(8,128)(2,1)S(1)} %get-tuple-element.53), channel_id=1, source_target_pairs={{0,1},{1,2},{2,3},{3,4},{4,5},{5,6},{6,7},{8,9},{9,10},{10,11},{11... | collective-permute-start | bytes 294920 | tf_op jit(solution)/shard_map/ppermute | solution.py:14
  67.3 4.6 %collective-permute-start.11 = (bf16[64,6,1,128]{3,0,2,1:T(8,128)(2,1)S(1)}, bf16[64,6,1,128]{3,0,2,1:T(8,128)(2,1)S(1)}, u32[]{:S(2)}, u32[]{:S(2)}) collective-permute-start(bf16[64,6,1,128]{3,0,2,1:T(8,128)(2,1)S(1)} %get-tuple-element.54), channel_id=1, source_target_pairs={{1,0},{2,1},{3,2},{4,3},{5,4},{6,5},{7,6},{9,8},{10,9},{11,10},{12... | collective-permute-start | bytes 294920 | tf_op jit(solution)/shard_map/ppermute | solution.py:15
  79.1 3.9 %copy-start.7 = (f32[1000,2]{0,1:T(2,128)S(1)}, f32[1000,2]{0,1:T(2,128)}, u32[]{:S(2)}) copy-start(f32[1000,2]{0,1:T(2,128)} %param.14) | copy-start | bytes 24004
  80.0 4.1 %collective-permute-start.12 = (bf16[64,1,8,128]{3,0,2,1:T(8,128)(2,1)S(1)}, bf16[64,1,8,128]{3,0,2,1:T(8,128)(2,1)S(1)}, u32[]{:S(2)}, u32[]{:S(2)}) collective-permute-start(bf16[64,1,8,128]{3,0,2,1:T(8,128)(2,1)S(1)} %get-tuple-element.57), channel_id=1, source_target_pairs={{0,8},{8,16},{16,24},{1,9},{9,17},{17,25},{2,10},{10,18},{18,26},{... | collective-permute-start | bytes 393224 | tf_op jit(solution)/shard_map/ppermute | solution.py:14
  81.6 6.9 %collective-permute-start.13 = (bf16[64,1,8,128]{3,0,2,1:T(8,128)(2,1)S(1)}, bf16[64,1,8,128]{3,0,2,1:T(8,128)(2,1)S(1)}, u32[]{:S(2)}, u32[]{:S(2)}) collective-permute-start(bf16[64,1,8,128]{3,0,2,1:T(8,128)(2,1)S(1)} %get-tuple-element.58), channel_id=1, source_target_pairs={{8,0},{16,8},{24,16},{9,1},{17,9},{25,17},{10,2},{18,10},{26,18},{... | collective-permute-start | bytes 393224 | tf_op jit(solution)/shard_map/ppermute | solution.py:15
  88.5 5.7 %collective-permute-start.14 = (bf16[64,6,1,128]{3,0,2,1:T(8,128)(2,1)S(1)}, bf16[64,6,1,128]{3,0,2,1:T(8,128)(2,1)S(1)}, u32[]{:S(2)}, u32[]{:S(2)}) collective-permute-start(bf16[64,6,1,128]{3,0,2,1:T(8,128)(2,1)S(1)} %get-tuple-element.51), channel_id=1, source_target_pairs={{0,1},{1,2},{2,3},{3,4},{4,5},{5,6},{6,7},{8,9},{9,10},{10,11},{11... | collective-permute-start | bytes 294920 | tf_op jit(solution)/shard_map/ppermute | solution.py:14
  92.3 4.3 %collective-permute-start.15 = (bf16[64,6,1,128]{3,0,2,1:T(8,128)(2,1)S(1)}, bf16[64,6,1,128]{3,0,2,1:T(8,128)(2,1)S(1)}, u32[]{:S(2)}, u32[]{:S(2)}) collective-permute-start(bf16[64,6,1,128]{3,0,2,1:T(8,128)(2,1)S(1)} %get-tuple-element.52), channel_id=1, source_target_pairs={{1,0},{2,1},{3,2},{4,3},{5,4},{6,5},{7,6},{9,8},{10,9},{11,10},{12... | collective-permute-start | bytes 294920 | tf_op jit(solution)/shard_map/ppermute | solution.py:15
  101.7 1.0 copy-start.2
  104.9 90.1 %copy-start.1 = (f32[8,4,8,128]{3,0,2,1:T(8,128)S(1)}, f32[8,4,8,128]{3,0,2,1:T(8,128)}, u32[]{:S(2)}) copy-start(f32[8,4,8,128]{3,0,2,1:T(8,128)} %fusion.53) | copy-start | bytes 393220
Sparse Core Ops, SparseCore 0:
  105.1 74.9 all-gather.2
where the time goes:
time: 204 us; the launch traced here: 203 us
  waiting for transfers between devices  106 us (52%)
  starting transfers between devices  33.7 us (17%)
  local copies, waits for them, and re-layouts  18.2 us (9%)
  matrix products  17.8 us (9%)
  between operations  15.3 us (8%)
  other arithmetic  10.6 us (5%)
    all_gather x1, waiting for transfers between devices, entering(): gathered = lax.all_gather(part, axis)  75.1 us
    ppermute x8, waiting for transfers between devices, with_halo(): after = lax.ppermute(leading, axis, down)  27.8 us
    ppermute x8, starting transfers between devices, with_halo(): before = lax.ppermute(last, axis, up)  23.2 us
    dot_general x36, matrix products, conv_valid(): jnp.einsum('czyx,cd->dzyx', window, taps, preferred_element_type=jnp.floa...  17.6 us
    dynamic_slice x15, local copies, waits for them, and re-layouts, one(): return combine(state, lax.dynamic_index_in_dim(gathered, step, 0, False))  13.8 us
    ppermute x8, starting transfers between devices, with_halo(): after = lax.ppermute(leading, axis, down)  10.5 us
    concatenate x4, other arithmetic, with_halo(): value = jnp.concatenate([before, value, after], axis=dim)  5.59 us
  transfers between devices with their start and end apart: 17, of which 12 were waited for; matrix products, arithmetic and copies ran while one was open for 1% of the time, Pallas kernels for 0%

commit v1 on v0

v1 whole, which is shorter than its diff:
```python
import functools

import jax
import jax.numpy as jnp
from jax import lax
from jax.experimental import pallas as pl
from jax.experimental.pallas import tpu as pltpu
from jax.sharding import PartitionSpec as P

F32 = jnp.float32
BF16 = jnp.bfloat16
DEPTH = 4


def banded(kernel, order):
    taps = jnp.transpose(kernel, (4, 1, 2, 0, 3))
    none = ((0, 0),) * 3
    first = jnp.pad(taps, none + ((0, 1), (0, 0)))
    second = jnp.pad(taps, none + ((1, 0), (0, 0)))
    return jnp.transpose(jnp.stack([first, second]), order)


def silu(x):
    return x / (1.0 + jnp.exp(-x))


def shifted(h):
    zero = jnp.zeros((h.shape[0], 1), h.dtype)
    left = jnp.concatenate([zero, h[:, :-1]], axis=1)
    right = jnp.concatenate([h[:, 1:], zero], axis=1)
    return left, h, right


def net_kernel(place, coef, x_ref, own_ref, bias_ref, w1_ref, w2_ref, w3_ref, w4_ref, out_ref, xs, h1, h2, h3):
    channels, nz, ny, nx = own_ref.shape
    hid = bias_ref.shape[0]
    z0, y0, z_size, y_size = place[0], place[1], place[2], place[3]

    def spread(rows, y):
        for d, v in enumerate(shifted(x_ref[y, rows, :])):
            xs[d, y, rows, :] = v

    for y in range(ny + 2 * DEPTH):
        spread(slice(None), y)

    def layer(src, w_ref, dst, depth, unit, dxs):
        off = DEPTH - depth
        pairs_z = (nz + 2 * off) // 2
        n_y = ny + 2 * off
        window = 4 * unit

        def step(zp, _):
            base = pl.multiple_of(zp * (2 * unit), 2 * unit)
            for y in range(0, n_y, 2):
                if depth == 1:
                    rhs = jnp.concatenate(
                        [
                            jnp.concatenate(
                                [src[dx, yy + dy, pl.ds(base, window), :] for dy in range(3) for dx in range(3)],
                                axis=0,
                            )
                            for yy in (y, y + 1)
                        ],
                        axis=1,
                    )
                    acc = jnp.dot(w_ref[...], rhs, preferred_element_type=F32)
                    acc = acc + jnp.tile(bias_ref[...], (2, 2))
                else:
                    acc = None
                    for k in range(9):
                        dy, dx = k // 3, k % 3
                        rhs = jnp.concatenate(
                            [src[dx, yy + dy, pl.ds(base, window), :] for yy in (y, y + 1)], axis=1
                        )
                        part = jnp.dot(
                            w_ref[:, k * window : (k + 1) * window], rhs, preferred_element_type=F32
                        )
                        acc = part if acc is None else acc + part
                h = silu(acc)
                for i in range(2):
                    gy = y0 - off + y + i
                    y_ok = jnp.logical_and(gy >= 0, gy < y_size)
                    for j in range(2):
                        gz = z0 - off + 2 * zp + j
                        ok = jnp.logical_and(y_ok, jnp.logical_and(gz >= 0, gz < z_size))
                        part = h[j * hid : (j + 1) * hid, i * nx : (i + 1) * nx]
                        part = jnp.where(ok, part, 0.0).astype(BF16)
                        rows = pl.ds(pl.multiple_of((2 * zp + j) * hid, hid), hid)
                        if dxs:
                            for d, v in enumerate(shifted(part)):
                                dst[d, y + i, rows, :] = v
                        else:
                            dst[y + i, rows, :] = part
            return 0

        lax.fori_loop(0, pairs_z, step, 0)

    layer(xs, w1_ref, h1, 1, channels, True)
    layer(h1, w2_ref, h2, 2, hid, True)
    layer(h2, w3_ref, h3, 3, hid, False)

    rows = 2 * channels
    lane = lax.broadcasted_iota(jnp.int32, (rows, nx), 1)
    a, b, first = coef[0], coef[1], coef[2]
    for zp in range(nz // 2):
        parts = []
        for y in range(0, ny + 2, 2):
            rhs = jnp.concatenate(
                [h3[yy, pl.ds(2 * zp * hid, 4 * hid), :] for yy in (y, y + 1)], axis=1
            )
            p = jnp.dot(w4_ref[...], rhs, preferred_element_type=F32)
            parts += [p[:, :nx], p[:, nx:]]
        nets = []
        for y in range(ny):
            t = [
                sum(parts[y + dy][(3 * dy + dx) * rows : (3 * dy + dx + 1) * rows] for dy in range(3))
                for dx in range(3)
            ]
            left = jnp.where(lane == 0, 0.0, pltpu.roll(t[0], 1, 1))
            right = jnp.where(lane == nx - 1, 0.0, pltpu.roll(t[2], nx - 1, 1))
            nets.append(left + t[1] + right)
        for j in range(2):
            net = jnp.stack([n[j * channels : (j + 1) * channels] for n in nets])
            net = jnp.transpose(net, (1, 0, 2))
            own = own_ref[:, 2 * zp + j]
            out_ref[:, 2 * zp + j] = b * net - a * own + first * own


def scan_kernel(d_ref, o_ref):
    total = d_ref[0]
    o_ref[0] = total
    for t in range(1, d_ref.shape[0]):
        total = total + d_ref[t]
        o_ref[t] = total


def vmem():
    return pl.BlockSpec(memory_space=pltpu.VMEM)


def smem():
    return pl.BlockSpec(memory_space=pltpu.SMEM)


def time_features(step, time_weight):
    half = time_weight.shape[0] // 2
    freqs = jnp.exp(-jnp.log(1000.0) * jnp.arange(half, dtype=F32) / half)
    angles = step.astype(F32) * freqs
    feats = jnp.concatenate([jnp.sin(angles), jnp.cos(angles)])
    return jnp.dot(feats, time_weight, precision=lax.Precision.HIGHEST)


def neighbours(value, axis):
    size = lax.axis_size(axis)
    up = [(i, i + 1) for i in range(size - 1)]
    down = [(j, i) for i, j in up]
    return (lambda v: lax.ppermute(v, axis, up)), (lambda v: lax.ppermute(v, axis, down))


def on_device(state, step_index, sched_index, coef_table, time_weight, w_in, w_mid1, w_mid2, w_out):
    own = state[0]
    channels, nz, ny, nx = own.shape
    hid = w_mid1.shape[3]
    slots = lax.axis_size("ta")

    x = jnp.transpose(own.astype(BF16), (2, 1, 0, 3))
    up, down = neighbours(x, "gz")
    x = jnp.concatenate([up(x), x, down(x)], axis=1)
    up, down = neighbours(x, "gy")
    x = jnp.concatenate([up(x[ny - DEPTH :]), x, down(x[:DEPTH])], axis=0)
    x = x.reshape(ny + 2 * DEPTH, (nz + 2 * DEPTH) * channels, nx)

    bias = jnp.broadcast_to(time_features(step_index[0], time_weight)[:, None], (hid, nx))
    ordered = (0, 1, 2, 3, 4, 5)
    w1 = banded(w_in, ordered).reshape(2 * hid, -1)
    w2 = banded(w_mid1, ordered).reshape(2 * hid, -1)
    w3 = banded(w_mid2, ordered).reshape(2 * hid, -1)
    w4 = banded(w_out, (2, 3, 0, 1, 4, 5)).reshape(9 * 2 * channels, -1)
    first = (lax.axis_index("ta") == 0).astype(F32)
    row = lax.dynamic_slice_in_dim(coef_table, sched_index[0], 1, 0)[0]
    coef = jnp.stack([row[0], row[1], first])
    place = jnp.stack(
        [
            lax.axis_index("gz") * nz,
            lax.axis_index("gy") * ny,
            jnp.int32(nz * lax.axis_size("gz")),
            jnp.int32(ny * lax.axis_size("gy")),
        ]
    ).astype(jnp.int32)

    drift = pl.pallas_call(
        net_kernel,
        out_shape=jax.ShapeDtypeStruct(own.shape, F32),
        in_specs=[smem(), smem()] + [vmem()] * 7,
        out_specs=vmem(),
        scratch_shapes=[
            pltpu.VMEM((3,) + x.shape, BF16),
            pltpu.VMEM((3, ny + 6, (nz + 6) * hid, nx), BF16),
            pltpu.VMEM((3, ny + 4, (nz + 4) * hid, nx), BF16),
            pltpu.VMEM((ny + 2, (nz + 2) * hid, nx), BF16),
        ],
        name="net",
    )(place, coef, x, own, bias, w1, w2, w3, w4)

    pieces = drift.reshape(slots, -1, nx)
    pieces = lax.all_to_all(pieces, "ta", 0, 0, tiled=True)
    sums = pl.pallas_call(
        scan_kernel,
        out_shape=jax.ShapeDtypeStruct(pieces.shape, F32),
        in_specs=[vmem()],
        out_specs=vmem(),
        name="scan",
    )(pieces)
    total = lax.all_to_all(sums, "ta", 0, 0, tiled=True)
    return total.reshape(own.shape)[None]


def solution(mesh):
    placed = (P("ta", None, "gz", "gy", None), P("ta"), P("ta"), P(), P(), P(), P(), P(), P())
    return jax.shard_map(
        on_device,
        mesh=mesh,
        in_specs=placed,
        out_specs=P("ta", None, "gz", "gy", None),
        check_vma=False,
    )
```

time: 204 us -> 97.5 us (0.48)
  the two profiles are of different devices: /device:TPU:480 before, /device:TPU:22 now
where the time goes in v1:
time: 97.5 us; the launch traced here: 97 us
  blocking collectives  49.9 us (51%)
  Pallas kernels  15.8 us (16%)
  local copies, waits for them, and re-layouts  12.2 us (13%)
  starting transfers between devices  11.4 us (12%)
  other arithmetic  4.34 us (4%)
  waiting for transfers between devices  1.63 us (2%)
  between operations  1.5 us (2%)
    all_to_all x1, blocking collectives, on_device(): pieces = lax.all_to_all(pieces, 'ta', 0, 0, tiled=True)  29 us
    all_to_all x1, blocking collectives, on_device(): total = lax.all_to_all(sums, 'ta', 0, 0, tiled=True)  20.9 us
    pallas_call x1, Pallas kernels, on_device(): pl.pallas_call(net_kernel, out_shape=jax.ShapeDtypeStruct(own.shape, F32)...  14.2 us
    ppermute x2, starting transfers between devices, neighbours(): lax.ppermute(v, axis, down)  8.19 us
    another operation x7, local copies, waits for them, and re-layouts, banded(): return jnp.transpose(jnp.stack([first, second]), order)  3.73 us
    ppermute x2, starting transfers between devices, neighbours(): lax.ppermute(v, axis, up)  3.21 us
    another operation x1, other arithmetic, on_device(): coef = jnp.stack([row[0], row[1], first])  1.96 us
  transfers between devices with their start and end apart: 4, of which 1 were waited for; matrix products, arithmetic and copies ran while one was open for 14% of the time, Pallas kernels for 0%

profile of v1, /device:TPU:22, one launch (start us, length us, event | category | flops | bytes accessed | tf_op | source)
XLA Modules:
  0.0 97.0 jit_solution(1279599562057997308)
XLA Ops:
  0.0 0.9 convert_bitcast_fusion
  0.9 1.3 %collective-permute-start = (bf16[8,4,8,128]{3,0,1,2:T(8,128)(2,1)S(1)}, bf16[8,4,8,128]{3,0,1,2:T(8,128)(2,1)S(1)}, u32[]{:S(2)}, u32[]{:S(2)}) collective-permute-start(bf16[8,4,8,128]{3,0,1,2:T(8,128)(2,1)S(1)} %convert_bitcast_fusion), channel_id=1, source_target_pairs={{0,8},{8,16},{16,24},{1,9},{9,17},{17,25},{2,10},{10,18},{18,26},{... | collective-permute-start | bytes 196616 | tf_op jit(solution)/shard_map/ppermute | solution.py:157
  2.2 4.5 %collective-permute-start.1 = (bf16[8,4,8,128]{3,0,1,2:T(8,128)(2,1)S(1)}, bf16[8,4,8,128]{3,0,1,2:T(8,128)(2,1)S(1)}, u32[]{:S(2)}, u32[]{:S(2)}) collective-permute-start(bf16[8,4,8,128]{3,0,1,2:T(8,128)(2,1)S(1)} %convert_bitcast_fusion), channel_id=1, source_target_pairs={{8,0},{16,8},{24,16},{9,1},{17,9},{25,17},{10,2},{18,10},{26,18},{... | collective-permute-start | bytes 196616 | tf_op jit(solution)/shard_map/ppermute | solution.py:157
  7.4 0.8 constant_dynamic-slice_fusion
  8.2 0.6 fusion.6
  8.8 1.4 %pad_bitcast_fusion.3 = (bf16[1,64,3,3,4,64]{1,5,3,2,4,0:T(8,128)(2,1)S(1)}, bf16[1,64,3,3,4,64]{1,5,3,2,4,0:T(8,128)(2,1)S(1)}) fusion(bf16[64,3,3,3,64]{0,4,2,1,3:T(8,128)(2,1)} %bitcast.53), kind=kLoop, calls=%fused_computation.6 | loop fusion | bytes 811008 | tf_op jit(solution)/shard_map/stack | solution.py:20
  10.2 0.3 pad_maximum_fusion
  10.5 0.9 copy.16
  11.5 1.5 %reshape.24.w2_ref = bf16[128,2304]{1,0:T(8,128)(2,1)} reshape(bf16[2,64,3,3,4,64]{5,4,3,2,1,0:T(4,128)(2,1)S(1)} %copy.16) | data formatting | bytes 1179648 | tf_op jit(solution)/shard_map/reshape | solution.py:176
  13.0 0.3 pad_bitcast_fusion.1
  13.2 0.3 pad_maximum_fusion.1
  13.5 0.9 copy.17
  14.5 1.5 %reshape.25.w3_ref = bf16[128,2304]{1,0:T(8,128)(2,1)} reshape(bf16[2,64,3,3,4,64]{5,4,3,2,1,0:T(4,128)(2,1)S(1)} %copy.17) | data formatting | bytes 1179648 | tf_op jit(solution)/shard_map/reshape | solution.py:177
  16.0 0.1 copy.15
  16.2 0.1 reshape.23
  16.3 0.7 copy.19.w1_ref
  17.2 0.8 reshape.26.w4_ref
  18.7 0.2 convolution_bitcast_fusion
  18.9 2.0 %pad_maximum_fusion.5.coef = f32[3]{0:T(128)} fusion(f32[1]{0:T(128)} %bitcast.5, f32[1]{0:T(128)} %bitcast.4, f32[1]{0:T(128)} %bitcast.3), kind=kLoop, calls=%fused_computation.18 | loop fusion | flops 6 | bytes 24 | tf_op jit(solution)/shard_map/stack | solution.py:181
  20.9 0.1 fusion.5
  21.0 1.9 %collective-permute-start.2 = (bf16[4,12,8,128]{3,0,1,2:T(4,128)(2,1)S(1)}, bf16[4,12,8,128]{3,0,1,2:T(4,128)(2,1)S(1)}, u32[]{:S(2)}, u32[]{:S(2)}) collective-permute-start(bf16[4,12,8,128]{3,0,1,2:T(4,128)(2,1)S(1)} %get-tuple-element.9), channel_id=1, source_target_pairs={{0,1},{1,2},{2,3},{3,4},{4,5},{5,6},{6,7},{8,9},{9,10},{10,11},{11... | collective-permute-start | bytes 294920 | tf_op jit(solution)/shard_map/ppermute | solution.py:157
  22.9 3.6 %collective-permute-start.3 = (bf16[4,12,8,128]{3,0,1,2:T(4,128)(2,1)S(1)}, bf16[4,12,8,128]{3,0,1,2:T(4,128)(2,1)S(1)}, u32[]{:S(2)}, u32[]{:S(2)}) collective-permute-start(bf16[4,12,8,128]{3,0,1,2:T(4,128)(2,1)S(1)} %get-tuple-element.10), channel_id=1, source_target_pairs={{1,0},{2,1},{3,2},{4,3},{5,4},{6,5},{7,6},{9,8},{10,9},{11,10},{12... | collective-permute-start | bytes 294920 | tf_op jit(solution)/shard_map/ppermute | solution.py:157
  26.5 0.6 pad_add_fusion.place
  27.1 1.6 %collective-permute-done.3 = bf16[4,12,8,128]{3,0,1,2:T(4,128)(2,1)S(1)} collective-permute-done((bf16[4,12,8,128]{3,0,1,2:T(4,128)(2,1)S(1)}, bf16[4,12,8,128]{3,0,1,2:T(4,128)(2,1)S(1)}, u32[]{:S(2)}, u32[]{:S(2)}) %collective-permute-start.3) | collective-permute-done | bytes 98336 | tf_op jit(solution)/shard_map/ppermute | solution.py:157
  28.7 0.2 pad_maximum_fusion.2
  29.0 1.0 %copy.21 = bf16[16,12,8,128]{3,2,1,0:T(8,128)(2,1)} copy(bf16[16,12,8,128]{3,0,1,2:T(8,128)(2,1)S(1)} %pad_maximum_fusion.2) | data formatting | bytes 786432 | tf_op jit(solution)/shard_map/concatenate | solution.py:170
  30.0 0.7 broadcast_in_dim.2.bias_ref
  30.7 14.2 %net.1 = f32[8,4,8,128]{3,2,1,0:T(8,128)} custom-call(s32[4]{0:T(128)} %pad_add_fusion.place, f32[3]{0:T(128)} %pad_maximum_fusion.5.coef, bf16[16,96,128]{2,1,0:T(8,128)(2,1)} %bitcast.49, f32[8,4,8,128]{3,2,1,0:T(8,128)} %bitcast.50, f32[64,128]{1,0:T(8,128)} %broadcast_in_dim.2.bias_ref, bf16[128,288]{1,0:T(8,128)(2,1)} %copy.19.w1_ref, ...), custom_call_target="tpu_custom_call" | custom-call | tf_op jit(solution)/shard_map/net/pallas_call | solution.py:191
  44.9 29.0 %all_to_all.10.d_ref = f32[16,16,128]{2,1,0:T(8,128)} all-to-all(f32[16,16,128]{2,1,0:T(8,128)} %bitcast.51), channel_id=1, replica_groups=mesh['ta'=16,'gz'=4,'gy'=8] {'ta'}, dimensions={0} | all-to-all | bytes 262144 | tf_op jit(solution)/shard_map/all_to_all | solution.py:206
  73.9 1.6 %scan.1 = f32[16,16,128]{2,1,0:T(8,128)} custom-call(f32[16,16,128]{2,1,0:T(8,128)} %all_to_all.10.d_ref), custom_call_target="tpu_custom_call" | custom-call | tf_op jit(solution)/shard_map/scan/pallas_call | solution.py:207
  75.5 20.9 %all_to_all.11 = f32[16,16,128]{2,1,0:T(8,128)S(1)} all-to-all(f32[16,16,128]{2,1,0:T(8,128)} %scan.1), channel_id=1, replica_groups=mesh['ta'=16,'gz'=4,'gy'=8] {'ta'}, dimensions={0} | all-to-all | bytes 262144 | tf_op jit(solution)/shard_map/all_to_all | solution.py:214
  96.4 0.7 copy.25
  (18 shorter events, 0.3 us)
Async XLA Ops:
  0.0 18.7 %copy-start = (f32[64,64]{1,0:T(8,128)S(1)}, f32[64,64]{1,0:T(8,128)}, u32[]{:S(2)}) copy-start(f32[64,64]{1,0:T(8,128)} %param.13) | copy-start | bytes 49156
  0.9 19.9 %collective-permute-start = (bf16[8,4,8,128]{3,0,1,2:T(8,128)(2,1)S(1)}, bf16[8,4,8,128]{3,0,1,2:T(8,128)(2,1)S(1)}, u32[]{:S(2)}, u32[]{:S(2)}) collective-permute-start(bf16[8,4,8,128]{3,0,1,2:T(8,128)(2,1)S(1)} %convert_bitcast_fusion), channel_id=1, source_target_pairs={{0,8},{8,16},{16,24},{1,9},{9,17},{17,25},{2,10},{10,18},{18,26},{... | collective-permute-start | bytes 196616 | tf_op jit(solution)/shard_map/ppermute | solution.py:157
  2.2 18.6 %collective-permute-start.1 = (bf16[8,4,8,128]{3,0,1,2:T(8,128)(2,1)S(1)}, bf16[8,4,8,128]{3,0,1,2:T(8,128)(2,1)S(1)}, u32[]{:S(2)}, u32[]{:S(2)}) collective-permute-start(bf16[8,4,8,128]{3,0,1,2:T(8,128)(2,1)S(1)} %convert_bitcast_fusion), channel_id=1, source_target_pairs={{8,0},{16,8},{24,16},{9,1},{17,9},{25,17},{10,2},{18,10},{26,18},{... | collective-permute-start | bytes 196616 | tf_op jit(solution)/shard_map/ppermute | solution.py:157
  11.4 1.5 %copy-start.1 = (bf16[3,3,3,64,64]{4,3,2,1,0:T(8,128)(2,1)S(1)}, bf16[3,3,3,64,64]{4,3,2,1,0:T(8,128)(2,1)}, u32[]{:S(2)}) copy-start(bf16[3,3,3,64,64]{4,3,2,1,0:T(8,128)(2,1)} %param.16) | copy-start | bytes 663556
  14.4 1.5 %copy-start.2 = (bf16[3,3,3,8,64]{4,3,2,1,0:T(8,128)(2,1)S(1)}, bf16[3,3,3,8,64]{4,3,2,1,0:T(8,128)(2,1)}, u32[]{:S(2)}) copy-start(bf16[3,3,3,8,64]{4,3,2,1,0:T(8,128)(2,1)} %param.14) | copy-start | bytes 82948
  14.5 2.6 %copy-start.3 = (bf16[3,3,3,64,8]{3,4,2,1,0:T(8,128)(2,1)S(1)}, bf16[3,3,3,64,8]{3,4,2,1,0:T(8,128)(2,1)}, u32[]{:S(2)}) copy-start(bf16[3,3,3,64,8]{3,4,2,1,0:T(8,128)(2,1)} %param.17) | copy-start | bytes 82948
  21.0 6.1 %collective-permute-start.2 = (bf16[4,12,8,128]{3,0,1,2:T(4,128)(2,1)S(1)}, bf16[4,12,8,128]{3,0,1,2:T(4,128)(2,1)S(1)}, u32[]{:S(2)}, u32[]{:S(2)}) collective-permute-start(bf16[4,12,8,128]{3,0,1,2:T(4,128)(2,1)S(1)} %get-tuple-element.9), channel_id=1, source_target_pairs={{0,1},{1,2},{2,3},{3,4},{4,5},{5,6},{6,7},{8,9},{9,10},{10,11},{11... | collective-permute-start | bytes 294920 | tf_op jit(solution)/shard_map/ppermute | solution.py:157
  22.9 5.8 %collective-permute-start.3 = (bf16[4,12,8,128]{3,0,1,2:T(4,128)(2,1)S(1)}, bf16[4,12,8,128]{3,0,1,2:T(4,128)(2,1)S(1)}, u32[]{:S(2)}, u32[]{:S(2)}) collective-permute-start(bf16[4,12,8,128]{3,0,1,2:T(4,128)(2,1)S(1)} %get-tuple-element.10), channel_id=1, source_target_pairs={{1,0},{2,1},{3,2},{4,3},{5,4},{6,5},{7,6},{9,8},{10,9},{11,10},{12... | collective-permute-start | bytes 294920 | tf_op jit(solution)/shard_map/ppermute | solution.py:157

commit v2 on v1

--- a/solution.py
+++ b/solution.py
@@ -12,12 +12,36 @@
 DEPTH = 4
 
 
-def banded(kernel, order):
-    taps = jnp.transpose(kernel, (4, 1, 2, 0, 3))
-    none = ((0, 0),) * 3
-    first = jnp.pad(taps, none + ((0, 1), (0, 0)))
-    second = jnp.pad(taps, none + ((1, 0), (0, 0)))
-    return jnp.transpose(jnp.stack([first, second]), order)
+def prep_kernel(sched, coef_ref, feats_ref, tw_ref, wi_ref, wa_ref, wb_ref, wo_ref, coef_o, bias_o, w1, w2, w3, w4):
+    def band(w_ref, k):
+        taps = [w_ref[dz, k // 3, k % 3] for dz in range(3)]
+        none = jnp.zeros_like(taps[0])
+        first = jnp.concatenate(taps + [none], axis=0)
+        second = jnp.concatenate([none] + taps, axis=0)
+        return jnp.concatenate([first, second], axis=1)
+
+    for k in range(9):
+        for w_ref, dst in ((wi_ref, w1), (wa_ref, w2), (wb_ref, w3)):
+            t = band(w_ref, k).T
+            dst[:, k * t.shape[1] : (k + 1) * t.shape[1]] = t
+        taps = [wo_ref[dz, k // 3, k % 3] for dz in range(3)]
+        none = jnp.zeros_like(taps[0])
+        both = [jnp.concatenate(taps + [none], axis=1), jnp.concatenate([none] + taps, axis=1)]
+        t = jnp.concatenate(both, axis=0)
+        w4[k * t.shape[0] : (k + 1) * t.shape[0], :] = t
+
+    hid = tw_ref.shape[0]
+    diag = lax.broadcasted_iota(jnp.int32, (hid, hid), 0) == lax.broadcasted_iota(jnp.int32, (hid, hid), 1)
+
+    def column(row):
+        return jnp.sum(jnp.where(diag, row, 0.0), axis=1, keepdims=True)
+
+    bias = jnp.sum(tw_ref[...] * column(feats_ref[...]), axis=0, keepdims=True)
+    bias_o[...] = jnp.broadcast_to(column(bias), bias_o.shape)
+    picked = lax.broadcasted_iota(jnp.int32, coef_ref.shape, 1) == sched[0]
+    both = jnp.sum(jnp.where(picked, coef_ref[...], 0.0), axis=1, keepdims=True)
+    for i in range(2):
+        coef_o[i] = jnp.broadcast_to(both[i : i + 1], coef_o.shape[1:])
 
 
 def silu(x):
@@ -31,17 +55,24 @@
     return left, h, right
 
 
-def net_kernel(place, coef, x_ref, own_ref, bias_ref, w1_ref, w2_ref, w3_ref, w4_ref, out_ref, xs, h1, h2, h3):
+def net_kernel(coef, x_ref, zb_ref, za_ref, yb_ref, ya_ref, own_ref, bias_ref, w1_ref, w2_ref, w3_ref, w4_ref, out_ref, xs, h1, h2, h3):
     channels, nz, ny, nx = own_ref.shape
     hid = bias_ref.shape[0]
-    z0, y0, z_size, y_size = place[0], place[1], place[2], place[3]
-
-    def spread(rows, y):
-        for d, v in enumerate(shifted(x_ref[y, rows, :])):
-            xs[d, y, rows, :] = v
-
-    for y in range(ny + 2 * DEPTH):
-        spread(slice(None), y)
+    z0, y0 = lax.axis_index("gz") * nz, lax.axis_index("gy") * ny
+    z_size, y_size = nz * lax.axis_size("gz"), ny * lax.axis_size("gy")
+
+    rows = nz * channels
+
+    def spread(v, y, start):
+        for d, v in enumerate(shifted(v)):
+            xs[d, y, start : start + v.shape[0], :] = v
+
+    for y in range(DEPTH):
+        spread(yb_ref[y], y, 0)
+        spread(ya_ref[y], ny + DEPTH + y, 0)
+    for y in range(ny):
+        for i, part in enumerate((zb_ref, x_ref, za_ref)):
+            spread(part[y], DEPTH + y, i * rows)
 
     def layer(src, w_ref, dst, depth, unit, dxs):
         off = DEPTH - depth
@@ -101,7 +132,8 @@
 
     rows = 2 * channels
     lane = lax.broadcasted_iota(jnp.int32, (rows, nx), 1)
-    a, b, first = coef[0], coef[1], coef[2]
+    a, b = coef[0], coef[1]
+    first = jnp.where(lax.axis_index("ta") == 0, 1.0, 0.0)
     for zp in range(nz // 2):
         parts = []
         for y in range(0, ny + 2, 2):
@@ -134,85 +166,116 @@
         o_ref[t] = total
 
 
+def add_kernel(d_ref, *refs):
+    *more, o_ref = refs
+    extra = more[0][...]
+    for ref in more[1:]:
+        extra = extra + ref[...]
+    for t in range(d_ref.shape[0]):
+        o_ref[t] = d_ref[t] + extra
+
+
+def entering(part, axis, team):
+    size = lax.axis_size(axis)
+    shape, nx = part.shape, part.shape[-1]
+    teams = [[first + i for i in range(team)] for first in range(0, size, team)]
+
+    def to(start, end):
+        return [(i, j) for i, j in zip(teams[start], teams[end])]
+
+    def swap(v):
+        return lax.all_to_all(v, axis, 0, 0, axis_index_groups=teams, tiled=True)
+
+    def local(kernel, shape, *values):
+        return pl.pallas_call(
+            kernel,
+            out_shape=pltpu.VMEM(shape, F32),
+            in_specs=[vmem()] * len(values),
+            out_specs=vmem(),
+        )(*held(*values))
+
+    pieces = swap(part.reshape(team, -1, nx))
+    sums = local(scan_kernel, pieces.shape, pieces)
+    total = sums[team - 1]
+    first = lax.ppermute(total, axis, to(0, 1))
+    third = lax.ppermute(total, axis, to(2, 3))
+    half = total + first
+    near = lax.ppermute(half, axis, to(1, 2))
+    far = lax.ppermute(half, axis, to(1, 3))
+    return swap(local(add_kernel, sums.shape, sums, first, third, near, far)).reshape(shape)
+
+
 def vmem():
     return pl.BlockSpec(memory_space=pltpu.VMEM)
 
 
-def smem():
-    return pl.BlockSpec(memory_space=pltpu.SMEM)
-
-
-def time_features(step, time_weight):
-    half = time_weight.shape[0] // 2
-    freqs = jnp.exp(-jnp.log(1000.0) * jnp.arange(half, dtype=F32) / half)
-    angles = step.astype(F32) * freqs
-    feats = jnp.concatenate([jnp.sin(angles), jnp.cos(angles)])
-    return jnp.dot(feats, time_weight, precision=lax.Precision.HIGHEST)
-
-
-def neighbours(value, axis):
-    size = lax.axis_size(axis)
-    up = [(i, i + 1) for i in range(size - 1)]
-    down = [(j, i) for i, j in up]
-    return (lambda v: lax.ppermute(v, axis, up)), (lambda v: lax.ppermute(v, axis, down))
-
-
-def on_device(state, step_index, sched_index, coef_table, time_weight, w_in, w_mid1, w_mid2, w_out):
-    own = state[0]
+def held(*values):
+    return [pltpu.with_memory_space_constraint(v, pltpu.VMEM) for v in values]
+
+
+def net_call(coef, x, zb, za, yb, ya, own, bias, w1, w2, w3, w4):
     channels, nz, ny, nx = own.shape
-    hid = w_mid1.shape[3]
-    slots = lax.axis_size("ta")
-
-    x = jnp.transpose(own.astype(BF16), (2, 1, 0, 3))
-    up, down = neighbours(x, "gz")
-    x = jnp.concatenate([up(x), x, down(x)], axis=1)
-    up, down = neighbours(x, "gy")
-    x = jnp.concatenate([up(x[ny - DEPTH :]), x, down(x[:DEPTH])], axis=0)
-    x = x.reshape(ny + 2 * DEPTH, (nz + 2 * DEPTH) * channels, nx)
-
-    bias = jnp.broadcast_to(time_features(step_index[0], time_weight)[:, None], (hid, nx))
-    ordered = (0, 1, 2, 3, 4, 5)
-    w1 = banded(w_in, ordered).reshape(2 * hid, -1)
-    w2 = banded(w_mid1, ordered).reshape(2 * hid, -1)
-    w3 = banded(w_mid2, ordered).reshape(2 * hid, -1)
-    w4 = banded(w_out, (2, 3, 0, 1, 4, 5)).reshape(9 * 2 * channels, -1)
-    first = (lax.axis_index("ta") == 0).astype(F32)
-    row = lax.dynamic_slice_in_dim(coef_table, sched_index[0], 1, 0)[0]
-    coef = jnp.stack([row[0], row[1], first])
-    place = jnp.stack(
-        [
-            lax.axis_index("gz") * nz,
-            lax.axis_index("gy") * ny,
-            jnp.int32(nz * lax.axis_size("gz")),
-            jnp.int32(ny * lax.axis_size("gy")),
-        ]
-    ).astype(jnp.int32)
-
-    drift = pl.pallas_call(
+    hid = bias.shape[0]
+    return pl.pallas_call(
         net_kernel,
-        out_shape=jax.ShapeDtypeStruct(own.shape, F32),
-        in_specs=[smem(), smem()] + [vmem()] * 7,
+        out_shape=pltpu.VMEM(own.shape, F32),
+        in_specs=[vmem()] * 12,
         out_specs=vmem(),
         scratch_shapes=[
-            pltpu.VMEM((3,) + x.shape, BF16),
+            pltpu.VMEM((3, ny + 2 * DEPTH, (nz + 2 * DEPTH) * channels, nx), BF16),
             pltpu.VMEM((3, ny + 6, (nz + 6) * hid, nx), BF16),
             pltpu.VMEM((3, ny + 4, (nz + 4) * hid, nx), BF16),
             pltpu.VMEM((ny + 2, (nz + 2) * hid, nx), BF16),
         ],
         name="net",
-    )(place, coef, x, own, bias, w1, w2, w3, w4)
-
-    pieces = drift.reshape(slots, -1, nx)
-    pieces = lax.all_to_all(pieces, "ta", 0, 0, tiled=True)
-    sums = pl.pallas_call(
-        scan_kernel,
-        out_shape=jax.ShapeDtypeStruct(pieces.shape, F32),
-        in_specs=[vmem()],
-        out_specs=vmem(),
-        name="scan",
-    )(pieces)
-    total = lax.all_to_all(sums, "ta", 0, 0, tiled=True)
-    return total.reshape(own.shape)[None]
+    )(*held(coef, x, zb, za, yb, ya), own, *held(bias, w1, w2, w3, w4))
+
+
+def features(step, half):
+    freqs = jnp.exp(-jnp.log(1000.0) * jnp.arange(half, dtype=F32) / half)
+    angles = step.astype(F32) * freqs
+    return jnp.concatenate([jnp.sin(angles), jnp.cos(angles)])
+
+
+def exchange(up, down, axis):
+    ahead = [(i, i + 1) for i in range(lax.axis_size(axis) - 1)]
+    return lax.ppermute(up, axis, ahead), lax.ppermute(down, axis, [(j, i) for i, j in ahead])
+
+
+def on_device(state, step_index, sched_index, coef_table, time_weight, w_in, w_mid1, w_mid2, w_out):
+    own = state[0]
+    channels, nz, ny, nx = own.shape
+    hid = w_mid1.shape[3]
+
+    x = jnp.transpose(own.astype(BF16), (2, 1, 0, 3)).reshape(ny, nz * channels, nx)
+    zb, za = exchange(x, x, "gz")
+    tall = [jnp.concatenate([v[part] for v in (zb, x, za)], axis=1) for part in (slice(ny - DEPTH, ny), slice(0, DEPTH))]
+    yb, ya = exchange(tall[0], tall[1], "gy")
+
+    feats = features(step_index[0], hid // 2)[None]
+    inputs = (feats, time_weight, w_in, w_mid1, w_mid2, jnp.swapaxes(w_out, 3, 4))
+    outputs = [
+        pltpu.VMEM(shape, dtype)
+        for shape, dtype in (
+            ((2, channels, nx), F32),
+            ((hid, nx), F32),
+            ((2 * hid, 36 * channels), BF16),
+            ((2 * hid, 36 * hid), BF16),
+            ((2 * hid, 36 * hid), BF16),
+            ((18 * channels, 4 * hid), BF16),
+        )
+    ]
+    coef, bias, w1, w2, w3, w4 = pl.pallas_call(
+        prep_kernel,
+        out_shape=outputs,
+        in_specs=[pl.BlockSpec(memory_space=pltpu.SMEM)] + [vmem()] * (1 + len(inputs)),
+        out_specs=[vmem()] * len(outputs),
+        name="prep",
+    )(sched_index, coef_table.T, *inputs)
+
+    drift = net_call(coef, x, zb, za, yb, ya, own, bias, w1, w2, w3, w4)
+
+    return entering(drift, "ta", 4)[None]
 
 
 def solution(mesh):

time: 97.5 us -> 69.6 us (0.71)
  the two profiles are of different devices: /device:TPU:22 before, /device:TPU:430 now
where the time goes in v2:
time: 69.6 us; the launch traced here: 69.2 us
  blocking collectives  18.2 us (26%)
  Pallas kernels  16.9 us (24%)
  waiting for transfers between devices  16.8 us (24%)
  starting transfers between devices  13.5 us (19%)
  other arithmetic  1.58 us (2%)
  between operations  1.49 us (2%)
  local copies, waits for them, and re-layouts  0.75 us (1%)
    all_to_all x2, blocking collectives, swap(): return lax.all_to_all(v, axis, 0, 0, axis_index_groups=teams, tiled=True)  18.2 us
    pallas_call x1, Pallas kernels, net_call(): pl.pallas_call(net_kernel, out_shape=pltpu.VMEM(own.shape, F32), in_specs...  13.4 us
    ppermute x1, waiting for transfers between devices, entering(): far = lax.ppermute(half, axis, to(1, 3))  6.95 us
    ppermute x1, waiting for transfers between devices, entering(): third = lax.ppermute(total, axis, to(2, 3))  6.42 us
    ppermute x2, starting transfers between devices, exchange(): lax.ppermute(down, axis, [(j, i) for i, j in ahead])  6.38 us
    pallas_call x1, Pallas kernels, on_device(): pl.pallas_call(prep_kernel, out_shape=outputs, in_specs=[pl.BlockSpec(mem...  3.49 us
    ppermute x2, waiting for transfers between devices, exchange(): lax.ppermute(up, axis, ahead)  3.41 us
    ppermute x2, starting transfers between devices, exchange(): lax.ppermute(up, axis, ahead)  3.21 us
  transfers between devices with their start and end apart: 8, of which 3 were waited for; matrix products, arithmetic and copies ran while one was open for 1% of the time, Pallas kernels for 5%

profile of v2, /device:TPU:430, one launch (start us, length us, event | category | flops | bytes accessed | tf_op | source)
XLA Modules:
  0.0 69.2 jit_solution(2113646983685647692)
XLA Ops:
  0.0 0.9 %convert_bitcast_fusion = bf16[8,4,8,128]{3,0,1,2:T(8,128)(2,1)S(1)} fusion(f32[1,8,4,8,128]{4,3,2,1,0:T(8,128)} %param.9), kind=kLoop, calls=%fused_computation.3 | loop fusion | flops 32768 | bytes 196608 | tf_op jit(solution)/shard_map/transpose | solution.py:250
  1.0 2.7 %collective-permute-start.1 = (bf16[8,32,128]{2,1,0:T(8,128)(2,1)S(1)}, bf16[8,32,128]{2,1,0:T(8,128)(2,1)S(1)}, u32[]{:S(2)}, u32[]{:S(2)}) collective-permute-start(bf16[8,32,128]{2,1,0:T(8,128)(2,1)S(1)} %bitcast.25), channel_id=1, source_target_pairs={{8,0},{16,8},{24,16},{9,1},{17,9},{25,17},{10,2},{18,10},{26,18},{... | collective-permute-start | bytes 196616 | tf_op jit(solution)/shard_map/ppermute | solution.py:242
  3.7 1.3 %collective-permute-start = (bf16[8,32,128]{2,1,0:T(8,128)(2,1)S(1)}, bf16[8,32,128]{2,1,0:T(8,128)(2,1)S(1)}, u32[]{:S(2)}, u32[]{:S(2)}) collective-permute-start(bf16[8,32,128]{2,1,0:T(8,128)(2,1)S(1)} %bitcast.26), channel_id=1, source_target_pairs={{0,8},{8,16},{16,24},{1,9},{9,17},{17,25},{2,10},{10,18},{18,26},{... | collective-permute-start | bytes 196616 | tf_op jit(solution)/shard_map/ppermute | solution.py:242
  6.4 0.1 fusion
  6.4 0.0 collective-permute-done.1.za_ref
  6.4 3.4 %collective-permute-done.zb_ref = bf16[8,32,128]{2,1,0:T(8,128)(2,1)S(1)} collective-permute-done((bf16[8,32,128]{2,1,0:T(8,128)(2,1)S(1)}, bf16[8,32,128]{2,1,0:T(8,128)(2,1)S(1)}, u32[]{:S(2)}, u32[]{:S(2)}) %collective-permute-start) | collective-permute-done | bytes 65568 | tf_op jit(solution)/shard_map/ppermute | solution.py:242
  9.9 1.9 %collective-permute-start.2 = (bf16[4,96,128]{2,1,0:T(8,128)(2,1)S(1)}, bf16[4,96,128]{2,1,0:T(8,128)(2,1)S(1)}, u32[]{:S(2)}, u32[]{:S(2)}) collective-permute-start(bf16[4,96,128]{2,1,0:T(8,128)(2,1)S(1)} %pad_maximum_fusion), channel_id=1, source_target_pairs={{0,1},{1,2},{2,3},{3,4},{4,5},{5,6},{6,7},{8,9},{9,10},{10,11},{11... | collective-permute-start | bytes 294920 | tf_op jit(solution)/shard_map/ppermute | solution.py:242
  11.8 3.6 %collective-permute-start.3 = (bf16[4,96,128]{2,1,0:T(8,128)(2,1)S(1)}, bf16[4,96,128]{2,1,0:T(8,128)(2,1)S(1)}, u32[]{:S(2)}, u32[]{:S(2)}) collective-permute-start(bf16[4,96,128]{2,1,0:T(8,128)(2,1)S(1)} %pad_maximum_fusion.1), channel_id=1, source_target_pairs={{1,0},{2,1},{3,2},{4,3},{5,4},{6,5},{7,6},{9,8},{10,9},{11,10},{12... | collective-permute-start | bytes 294920 | tf_op jit(solution)/shard_map/ppermute | solution.py:242
  15.5 0.6 maximum_bitcast_fusion.feats_ref
  16.1 3.5 %prep.1 = (f32[2,8,128]{2,1,0:T(8,128)S(1)}, f32[64,128]{1,0:T(8,128)S(1)}, bf16[128,288]{1,0:T(8,128)(2,1)S(1)}, bf16[128,2304]{1,0:T(8,128)(2,1)S(1)}, bf16[12...) custom-call(s32[1]{0:T(128)S(6)} %copy.21.sched, f32[2,1000]{1,0:T(2,128)} %bitcast.33, ...), custom_call_target="tpu_custom_call" | custom-call | tf_op jit(solution)/shard_map/prep/pallas_call | solution.py:268
  19.6 0.0 collective-permute-done.2.yb_ref
  19.6 0.0 collective-permute-done.3.ya_ref
  19.6 13.4 %net.1 = f32[8,4,8,128]{3,2,1,0:T(8,128)S(1)} custom-call(f32[2,8,128]{2,1,0:T(8,128)S(1)} %get-tuple-element.11.coef, bf16[8,32,128]{2,1,0:T(8,128)(2,1)S(1)} %bitcast.27, bf16[8,32,128]{2,1,0:T(8,128)(2,1)S(1)} %collective-permute-done.zb_ref, bf16[8,32,128]{2,1,0:T(8,128)(2,1)S(1)} %collective-permute-done.1.za_ref, ...), custom_call_target="tpu_custom_call" | custom-call | tf_op jit(solution)/shard_map/net/pallas_call | solution.py:219
  33.0 9.2 %all_to_all.10.d_ref = f32[4,64,128]{2,1,0:T(8,128)S(1)} all-to-all(f32[4,64,128]{2,1,0:T(8,128)S(1)} %bitcast.24), channel_id=1, replica_groups={{0,32,64,96},{128,160,192,224},{256,288,320,352},{384,416,448,480},{1,3..., dimensions={0} | all-to-all | bytes 262144 | tf_op jit(solution)/shard_map/all_to_all | solution.py:187
  42.2 0.7 collective-permute-start.4
  42.8 1.3 %collective-permute-start.5 = (f32[64,128]{1,0:T(8,128)S(1)}, f32[64,128]{1,0:T(8,128)S(1)}, u32[]{:S(2)}, u32[]{:S(2)}) collective-permute-start(f32[64,128]{1,0:T(8,128)S(1)} %slice_bitcast_fusion), channel_id=1, source_target_pairs={{256,384},{288,416},{320,448},{352,480},{257,385},{289,417},{321,4... | collective-permute-start | bytes 98312 | tf_op jit(solution)/shard_map/ppermute | solution.py:201
  44.1 0.0 collective-permute-done.4.refs_0_
  44.2 1.3 %collective-permute-start.7 = (f32[64,128]{1,0:T(8,128)S(1)}, f32[64,128]{1,0:T(8,128)S(1)}, u32[]{:S(2)}, u32[]{:S(2)}) collective-permute-start(f32[64,128]{1,0:T(8,128)S(1)} %fusion.2), channel_id=1, source_target_pairs={{128,384},{160,416},{192,448},{224,480},{129,385},{161,417},{193,4... | collective-permute-start | bytes 98312 | tf_op jit(solution)/shard_map/ppermute | solution.py:204
  45.5 0.7 collective-permute-start.6
  46.1 6.4 %collective-permute-done.5.refs_1_ = f32[64,128]{1,0:T(8,128)S(1)} collective-permute-done((f32[64,128]{1,0:T(8,128)S(1)}, f32[64,128]{1,0:T(8,128)S(1)}, u32[]{:S(2)}, u32[]{:S(2)}) %collective-permute-start.5) | collective-permute-done | bytes 32800 | tf_op jit(solution)/shard_map/ppermute | solution.py:201
  52.6 7.0 %collective-permute-done.7.refs_3_ = f32[64,128]{1,0:T(8,128)S(1)} collective-permute-done((f32[64,128]{1,0:T(8,128)S(1)}, f32[64,128]{1,0:T(8,128)S(1)}, u32[]{:S(2)}, u32[]{:S(2)}) %collective-permute-start.7) | collective-permute-done | bytes 32800 | tf_op jit(solution)/shard_map/ppermute | solution.py:204
  59.5 0.0 collective-permute-done.6.refs_2_
  59.5 9.0 %all_to_all.11 = f32[4,64,128]{2,1,0:T(8,128)S(1)} all-to-all(f32[4,64,128]{2,1,0:T(8,128)S(1)} %shard_map.92), channel_id=1, replica_groups={{0,32,64,96},{128,160,192,224},{256,288,320,352},{384,416,448,480},{1,3..., dimensions={0} | all-to-all | bytes 262144 | tf_op jit(solution)/shard_map/all_to_all | solution.py:187
  68.6 0.7 copy.22
  (12 shorter events, 0.1 us)
Async XLA Ops:
  1.0 5.5 %collective-permute-start.1 = (bf16[8,32,128]{2,1,0:T(8,128)(2,1)S(1)}, bf16[8,32,128]{2,1,0:T(8,128)(2,1)S(1)}, u32[]{:S(2)}, u32[]{:S(2)}) collective-permute-start(bf16[8,32,128]{2,1,0:T(8,128)(2,1)S(1)} %bitcast.25), channel_id=1, source_target_pairs={{8,0},{16,8},{24,16},{9,1},{17,9},{25,17},{10,2},{18,10},{26,18},{... | collective-permute-start | bytes 196616 | tf_op jit(solution)/shard_map/ppermute | solution.py:242
  3.7 6.2 %collective-permute-start = (bf16[8,32,128]{2,1,0:T(8,128)(2,1)S(1)}, bf16[8,32,128]{2,1,0:T(8,128)(2,1)S(1)}, u32[]{:S(2)}, u32[]{:S(2)}) collective-permute-start(bf16[8,32,128]{2,1,0:T(8,128)(2,1)S(1)} %bitcast.26), channel_id=1, source_target_pairs={{0,8},{8,16},{16,24},{1,9},{9,17},{17,25},{2,10},{10,18},{18,26},{... | collective-permute-start | bytes 196616 | tf_op jit(solution)/shard_map/ppermute | solution.py:242
  9.9 9.7 %collective-permute-start.2 = (bf16[4,96,128]{2,1,0:T(8,128)(2,1)S(1)}, bf16[4,96,128]{2,1,0:T(8,128)(2,1)S(1)}, u32[]{:S(2)}, u32[]{:S(2)}) collective-permute-start(bf16[4,96,128]{2,1,0:T(8,128)(2,1)S(1)} %pad_maximum_fusion), channel_id=1, source_target_pairs={{0,1},{1,2},{2,3},{3,4},{4,5},{5,6},{6,7},{8,9},{9,10},{10,11},{11... | collective-permute-start | bytes 294920 | tf_op jit(solution)/shard_map/ppermute | solution.py:242
  11.8 7.8 %collective-permute-start.3 = (bf16[4,96,128]{2,1,0:T(8,128)(2,1)S(1)}, bf16[4,96,128]{2,1,0:T(8,128)(2,1)S(1)}, u32[]{:S(2)}, u32[]{:S(2)}) collective-permute-start(bf16[4,96,128]{2,1,0:T(8,128)(2,1)S(1)} %pad_maximum_fusion.1), channel_id=1, source_target_pairs={{1,0},{2,1},{3,2},{4,3},{5,4},{6,5},{7,6},{9,8},{10,9},{11,10},{12... | collective-permute-start | bytes 294920 | tf_op jit(solution)/shard_map/ppermute | solution.py:242
  42.2 2.0 %collective-permute-start.4 = (f32[64,128]{1,0:T(8,128)S(1)}, f32[64,128]{1,0:T(8,128)S(1)}, u32[]{:S(2)}, u32[]{:S(2)}) collective-permute-start(f32[64,128]{1,0:T(8,128)S(1)} %slice_bitcast_fusion), channel_id=1, source_target_pairs={{0,128},{32,160},{64,192},{96,224},{1,129},{33,161},{65,193},{97,2... | collective-permute-start | bytes 98312 | tf_op jit(solution)/shard_map/ppermute | solution.py:200
  42.8 9.7 %collective-permute-start.5 = (f32[64,128]{1,0:T(8,128)S(1)}, f32[64,128]{1,0:T(8,128)S(1)}, u32[]{:S(2)}, u32[]{:S(2)}) collective-permute-start(f32[64,128]{1,0:T(8,128)S(1)} %slice_bitcast_fusion), channel_id=1, source_target_pairs={{256,384},{288,416},{320,448},{352,480},{257,385},{289,417},{321,4... | collective-permute-start | bytes 98312 | tf_op jit(solution)/shard_map/ppermute | solution.py:201
  44.2 15.3 %collective-permute-start.7 = (f32[64,128]{1,0:T(8,128)S(1)}, f32[64,128]{1,0:T(8,128)S(1)}, u32[]{:S(2)}, u32[]{:S(2)}) collective-permute-start(f32[64,128]{1,0:T(8,128)S(1)} %fusion.2), channel_id=1, source_target_pairs={{128,384},{160,416},{192,448},{224,480},{129,385},{161,417},{193,4... | collective-permute-start | bytes 98312 | tf_op jit(solution)/shard_map/ppermute | solution.py:204
  45.5 14.0 %collective-permute-start.6 = (f32[64,128]{1,0:T(8,128)S(1)}, f32[64,128]{1,0:T(8,128)S(1)}, u32[]{:S(2)}, u32[]{:S(2)}) collective-permute-start(f32[64,128]{1,0:T(8,128)S(1)} %fusion.2), channel_id=1, source_target_pairs={{128,256},{160,288},{192,320},{224,352},{129,257},{161,289},{193,3... | collective-permute-start | bytes 98312 | tf_op jit(solution)/shard_map/ppermute | solution.py:203

commit v3 on v2

--- a/solution.py
+++ b/solution.py
@@ -20,9 +20,16 @@
         second = jnp.concatenate([none] + taps, axis=0)
         return jnp.concatenate([first, second], axis=1)
 
+    def flipped(v):
+        n = v.shape[1]
+        unit = (
+            lax.broadcasted_iota(jnp.int32, (n, n), 0) == lax.broadcasted_iota(jnp.int32, (n, n), 1)
+        ).astype(BF16)
+        return lax.dot_general(unit, v, (((1,), (1,)), ((), ())), preferred_element_type=F32).astype(BF16)
+
     for k in range(9):
         for w_ref, dst in ((wi_ref, w1), (wa_ref, w2), (wb_ref, w3)):
-            t = band(w_ref, k).T
+            t = flipped(band(w_ref, k))
             dst[:, k * t.shape[1] : (k + 1) * t.shape[1]] = t
         taps = [wo_ref[dz, k // 3, k % 3] for dz in range(3)]
         none = jnp.zeros_like(taps[0])
@@ -67,12 +74,19 @@
         for d, v in enumerate(shifted(v)):
             xs[d, y, start : start + v.shape[0], :] = v
 
+    def ordered(odd, first, second):
+        first, second = first.astype(F32), second.astype(F32)
+        return jnp.where(odd, first, second).astype(BF16), jnp.where(odd, second, first).astype(BF16)
+
+    odd_y, odd_z = is_odd("gy"), is_odd("gz")
     for y in range(DEPTH):
-        spread(yb_ref[y], y, 0)
-        spread(ya_ref[y], ny + DEPTH + y, 0)
+        before, after = ordered(odd_y, yb_ref[y], ya_ref[y])
+        spread(before, y, 0)
+        spread(after, ny + DEPTH + y, 0)
     for y in range(ny):
-        for i, part in enumerate((zb_ref, x_ref, za_ref)):
-            spread(part[y], DEPTH + y, i * rows)
+        before, after = ordered(odd_z, zb_ref[y], za_ref[y])
+        for i, part in enumerate((before, x_ref[y], after)):
+            spread(part, DEPTH + y, i * rows)
 
     def layer(src, w_ref, dst, depth, unit, dxs):
         off = DEPTH - depth
@@ -124,7 +138,7 @@
                             dst[y + i, rows, :] = part
             return 0
 
-        lax.fori_loop(0, pairs_z, step, 0)
+        lax.fori_loop(0, pairs_z, step, 0, unroll=True)
 
     layer(xs, w1_ref, h1, 1, channels, True)
     layer(h1, w2_ref, h2, 2, hid, True)
@@ -198,11 +212,10 @@
     sums = local(scan_kernel, pieces.shape, pieces)
     total = sums[team - 1]
     first = lax.ppermute(total, axis, to(0, 1))
-    third = lax.ppermute(total, axis, to(2, 3))
     half = total + first
-    near = lax.ppermute(half, axis, to(1, 2))
     far = lax.ppermute(half, axis, to(1, 3))
-    return swap(local(add_kernel, sums.shape, sums, first, third, near, far)).reshape(shape)
+    near = lax.ppermute(half, axis, to(1, 2) + to(2, 3))
+    return swap(local(add_kernel, sums.shape, sums, first, near, far)).reshape(shape)
 
 
 def vmem():
@@ -227,6 +240,7 @@
             pltpu.VMEM((3, ny + 4, (nz + 4) * hid, nx), BF16),
             pltpu.VMEM((ny + 2, (nz + 2) * hid, nx), BF16),
         ],
+        compiler_params=pltpu.CompilerParams(vmem_limit_bytes=24 << 20),
         name="net",
     )(*held(coef, x, zb, za, yb, ya), own, *held(bias, w1, w2, w3, w4))
 
@@ -237,9 +251,18 @@
     return jnp.concatenate([jnp.sin(angles), jnp.cos(angles)])
 
 
+def is_odd(axis):
+    return lax.rem(lax.axis_index(axis), 2) == 1
+
+
 def exchange(up, down, axis):
-    ahead = [(i, i + 1) for i in range(lax.axis_size(axis) - 1)]
-    return lax.ppermute(up, axis, ahead), lax.ppermute(down, axis, [(j, i) for i, j in ahead])
+    size = lax.axis_size(axis)
+    got = []
+    for start in (0, 1):
+        pairs = [(i, i + 1) for i in range(start, size - 1, 2)]
+        send = up if up is down else jnp.where(is_odd(axis) == (start == 1), up, down)
+        got.append(lax.ppermute(send, axis, pairs + [(j, i) for i, j in pairs]))
+    return got
 
 
 def on_device(state, step_index, sched_index, coef_table, time_weight, w_in, w_mid1, w_mid2, w_out):
@@ -249,7 +272,9 @@
 
     x = jnp.transpose(own.astype(BF16), (2, 1, 0, 3)).reshape(ny, nz * channels, nx)
     zb, za = exchange(x, x, "gz")
-    tall = [jnp.concatenate([v[part] for v in (zb, x, za)], axis=1) for part in (slice(ny - DEPTH, ny), slice(0, DEPTH))]
+    odd = is_odd("gz")
+    column = (jnp.where(odd, zb, za), x, jnp.where(odd, za, zb))
+    tall = [jnp.concatenate([v[part] for v in column], axis=1) for part in (slice(ny - DEPTH, ny), slice(0, DEPTH))]
     yb, ya = exchange(tall[0], tall[1], "gy")
 
     feats = features(step_index[0], hid // 2)[None]
@@ -270,8 +295,9 @@
         out_shape=outputs,
         in_specs=[pl.BlockSpec(memory_space=pltpu.SMEM)] + [vmem()] * (1 + len(inputs)),
         out_specs=[vmem()] * len(outputs),
+        compiler_params=pltpu.CompilerParams(vmem_limit_bytes=8 << 20),
         name="prep",
-    )(sched_index, coef_table.T, *inputs)
+    )(sched_index, *held(coef_table.T, *inputs))
 
     drift = net_call(coef, x, zb, za, yb, ya, own, bias, w1, w2, w3, w4)
 

time: 69.6 us -> 64 us (0.920)
  the two profiles are of different devices: /device:TPU:430 before, /device:TPU:426 now
where the time goes in v3:
time: 64 us; the launch traced here: 63.6 us
  blocking collectives  18.4 us (29%)
  waiting for transfers between devices  16.9 us (26%)
  starting transfers between devices  14.1 us (22%)
  Pallas kernels  10.7 us (17%)
  between operations  1.56 us (2%)
  other arithmetic  1.11 us (2%)
  local copies, waits for them, and re-layouts  0.88 us (1%)
    all_to_all x2, blocking collectives, swap(): return lax.all_to_all(v, axis, 0, 0, axis_index_groups=teams, tiled=True)  18.4 us
    ppermute x1, waiting for transfers between devices, entering(): far = lax.ppermute(half, axis, to(1, 3))  14.1 us
    ppermute x4, starting transfers between devices, exchange(): got.append(lax.ppermute(send, axis, pairs + [(j, i) for i, j in pairs]))  10.8 us
    pallas_call x1, Pallas kernels, net_call(): pl.pallas_call(net_kernel, out_shape=pltpu.VMEM(own.shape, F32), in_specs...  9.9 us
    ppermute x4, waiting for transfers between devices, exchange(): got.append(lax.ppermute(send, axis, pairs + [(j, i) for i, j in pairs]))  2.78 us
    ppermute x1, starting transfers between devices, entering(): far = lax.ppermute(half, axis, to(1, 3))  1.29 us
    ppermute x1, starting transfers between devices, entering(): near = lax.ppermute(half, axis, to(1, 2) + to(2, 3))  1.29 us
  transfers between devices with their start and end apart: 7, of which 2 were waited for; matrix products, arithmetic and copies ran while one was open for 0% of the time, Pallas kernels for 1%

profile of v3, /device:TPU:426, one launch (start us, length us, event | category | flops | bytes accessed | tf_op | source)
XLA Modules:
  0.0 63.6 jit_solution(11788660066646762466)
XLA Ops:
  0.0 0.9 %convert_bitcast_fusion = bf16[8,4,8,128]{3,0,1,2:T(8,128)(2,1)S(1)} fusion(f32[1,8,4,8,128]{4,3,2,1,0:T(8,128)} %param.9), kind=kLoop, calls=%fused_computation.5 | loop fusion | flops 32768 | bytes 196608 | tf_op jit(solution)/shard_map/transpose | solution.py:273
  1.0 3.4 %collective-permute-start.1 = (bf16[8,32,128]{2,1,0:T(8,128)(2,1)S(1)}, bf16[8,32,128]{2,1,0:T(8,128)(2,1)S(1)}, u32[]{:S(2)}, u32[]{:S(2)}) collective-permute-start(bf16[8,32,128]{2,1,0:T(8,128)(2,1)S(1)} %bitcast.24), channel_id=1, source_target_pairs={{8,16},{16,8},{9,17},{17,9},{10,18},{18,10},{11,19},{19,11},{12,20... | collective-permute-start | bytes 196616 | tf_op jit(solution)/shard_map/ppermute | solution.py:264
  4.4 1.9 %collective-permute-start = (bf16[8,32,128]{2,1,0:T(8,128)(2,1)S(1)}, bf16[8,32,128]{2,1,0:T(8,128)(2,1)S(1)}, u32[]{:S(2)}, u32[]{:S(2)}) collective-permute-start(bf16[8,32,128]{2,1,0:T(8,128)(2,1)S(1)} %bitcast.25), channel_id=1, source_target_pairs={{0,8},{16,24},{8,0},{24,16},{1,9},{17,25},{9,1},{25,17},{2,10},{18... | collective-permute-start | bytes 196616 | tf_op jit(solution)/shard_map/ppermute | solution.py:264
  7.6 0.0 copy-start.4
  7.6 0.0 copy-start.5
  7.7 0.0 copy-start.6
  7.7 0.1 fusion
  7.8 0.0 copy-start.1
  7.8 0.0 copy-start.2
  7.8 0.0 collective-permute-done.1.za_ref
  7.8 2.7 %collective-permute-done.zb_ref = bf16[8,32,128]{2,1,0:T(8,128)(2,1)S(1)} collective-permute-done((bf16[8,32,128]{2,1,0:T(8,128)(2,1)S(1)}, bf16[8,32,128]{2,1,0:T(8,128)(2,1)S(1)}, u32[]{:S(2)}, u32[]{:S(2)}) %collective-permute-start) | collective-permute-done | bytes 65568 | tf_op jit(solution)/shard_map/ppermute | solution.py:264
  10.6 0.0 copy-start.3
  10.6 1.9 %collective-permute-start.3 = (bf16[4,96,128]{2,1,0:T(8,128)(2,1)S(1)}, bf16[4,96,128]{2,1,0:T(8,128)(2,1)S(1)}, u32[]{:S(2)}, u32[]{:S(2)}) collective-permute-start(bf16[4,96,128]{2,1,0:T(8,128)(2,1)S(1)} %get-tuple-element.17), channel_id=1, source_target_pairs={{1,2},{3,4},{5,6},{2,1},{4,3},{6,5},{9,10},{11,12},{13,14},{10,9},... | collective-permute-start | bytes 294920 | tf_op jit(solution)/shard_map/ppermute | solution.py:264
  12.6 3.6 %collective-permute-start.2 = (bf16[4,96,128]{2,1,0:T(8,128)(2,1)S(1)}, bf16[4,96,128]{2,1,0:T(8,128)(2,1)S(1)}, u32[]{:S(2)}, u32[]{:S(2)}) collective-permute-start(bf16[4,96,128]{2,1,0:T(8,128)(2,1)S(1)} %get-tuple-element.18), channel_id=1, source_target_pairs={{0,1},{2,3},{4,5},{6,7},{1,0},{3,2},{5,4},{7,6},{8,9},{10,11},{12,... | collective-permute-start | bytes 294920 | tf_op jit(solution)/shard_map/ppermute | solution.py:264
  16.1 0.1 maximum_bitcast_fusion.feats_ref
  16.2 0.0 copy-done.6
  16.2 0.0 copy-done.2
  16.3 0.0 copy-start
  16.3 0.7 %prep.1 = (f32[2,8,128]{2,1,0:T(8,128)S(1)}, f32[64,128]{1,0:T(8,128)S(1)}, bf16[128,288]{1,0:T(8,128)(2,1)S(1)}, bf16[128,2304]{1,0:T(8,128)(2,1)S(1)}, bf16[12...) custom-call(s32[1]{0:T(128)S(6)} %copy.19.sched, f32[2,1000]{1,0:T(2,128)S(1)} %bitcast.28, ...), custom_call_target="tpu_custom_call" | custom-call | tf_op jit(solution)/shard_map/prep/pallas_call | solution.py:293
  17.0 0.0 collective-permute-done.3.ya_ref
  17.0 0.0 collective-permute-done.2.yb_ref
  17.1 0.1 copy-done
  17.2 9.9 %net.1 = f32[8,4,8,128]{3,2,1,0:T(8,128)S(1)} custom-call(f32[2,8,128]{2,1,0:T(8,128)S(1)} %get-tuple-element.11.coef, bf16[8,32,128]{2,1,0:T(8,128)(2,1)S(1)} %bitcast.26, bf16[8,32,128]{2,1,0:T(8,128)(2,1)S(1)} %collective-permute-done.zb_ref, bf16[8,32,128]{2,1,0:T(8,128)(2,1)S(1)} %collective-permute-done.1.za_ref, ...), custom_call_target="tpu_custom_call" | custom-call | tf_op jit(solution)/shard_map/net/pallas_call | solution.py:232
  27.1 9.2 %all_to_all.10.d_ref = f32[4,64,128]{2,1,0:T(8,128)S(1)} all-to-all(f32[4,64,128]{2,1,0:T(8,128)S(1)} %bitcast.23), channel_id=1, replica_groups={{0,32,64,96},{128,160,192,224},{256,288,320,352},{384,416,448,480},{1,3..., dimensions={0} | all-to-all | bytes 262144 | tf_op jit(solution)/shard_map/all_to_all | solution.py:201
  36.3 0.7 %collective-permute-start.4 = (f32[64,128]{1,0:T(8,128)S(1)}, f32[64,128]{1,0:T(8,128)S(1)}, u32[]{:S(2)}, u32[]{:S(2)}) collective-permute-start(f32[64,128]{1,0:T(8,128)S(1)} %slice_bitcast_fusion), channel_id=1, source_target_pairs={{0,128},{32,160},{64,192},{96,224},{1,129},{33,161},{65,193},{97,2... | collective-permute-start | bytes 98312 | tf_op jit(solution)/shard_map/ppermute | solution.py:214
  37.0 0.0 collective-permute-done.4.refs_0_
  37.0 1.3 %collective-permute-start.6 = (f32[64,128]{1,0:T(8,128)S(1)}, f32[64,128]{1,0:T(8,128)S(1)}, u32[]{:S(2)}, u32[]{:S(2)}) collective-permute-start(f32[64,128]{1,0:T(8,128)S(1)} %fusion.2), channel_id=1, source_target_pairs={{128,384},{160,416},{192,448},{224,480},{129,385},{161,417},{193,4... | collective-permute-start | bytes 98312 | tf_op jit(solution)/shard_map/ppermute | solution.py:216
  38.3 1.3 %collective-permute-start.5 = (f32[64,128]{1,0:T(8,128)S(1)}, f32[64,128]{1,0:T(8,128)S(1)}, u32[]{:S(2)}, u32[]{:S(2)}) collective-permute-start(f32[64,128]{1,0:T(8,128)S(1)} %fusion.2), channel_id=1, source_target_pairs={{128,256},{160,288},{192,320},{224,352},{256,384},{288,416},{320,4... | collective-permute-start | bytes 98312 | tf_op jit(solution)/shard_map/ppermute | solution.py:217
  39.6 14.1 %collective-permute-done.6.refs_2_ = f32[64,128]{1,0:T(8,128)S(1)} collective-permute-done((f32[64,128]{1,0:T(8,128)S(1)}, f32[64,128]{1,0:T(8,128)S(1)}, u32[]{:S(2)}, u32[]{:S(2)}) %collective-permute-start.6) | collective-permute-done | bytes 32800 | tf_op jit(solution)/shard_map/ppermute | solution.py:216
  53.7 0.0 collective-permute-done.5.refs_1_
  53.8 9.2 %all_to_all.11 = f32[4,64,128]{2,1,0:T(8,128)S(1)} all-to-all(f32[4,64,128]{2,1,0:T(8,128)S(1)} %shard_map.92), channel_id=1, replica_groups={{0,32,64,96},{128,160,192,224},{256,288,320,352},{384,416,448,480},{1,3..., dimensions={0} | all-to-all | bytes 262144 | tf_op jit(solution)/shard_map/all_to_all | solution.py:201
  62.9 0.7 %copy.20 = f32[1,8,4,8,128]{4,3,2,1,0:T(8,128)} copy(f32[1,8,4,8,128]{4,3,2,1,0:T(8,128)S(1)} %bitcast.29) | data formatting | bytes 262144
  (14 shorter events, 0.2 us)
Async XLA Ops:
  1.0 6.8 %collective-permute-start.1 = (bf16[8,32,128]{2,1,0:T(8,128)(2,1)S(1)}, bf16[8,32,128]{2,1,0:T(8,128)(2,1)S(1)}, u32[]{:S(2)}, u32[]{:S(2)}) collective-permute-start(bf16[8,32,128]{2,1,0:T(8,128)(2,1)S(1)} %bitcast.24), channel_id=1, source_target_pairs={{8,16},{16,8},{9,17},{17,9},{10,18},{18,10},{11,19},{19,11},{12,20... | collective-permute-start | bytes 196616 | tf_op jit(solution)/shard_map/ppermute | solution.py:264
  4.4 6.2 %collective-permute-start = (bf16[8,32,128]{2,1,0:T(8,128)(2,1)S(1)}, bf16[8,32,128]{2,1,0:T(8,128)(2,1)S(1)}, u32[]{:S(2)}, u32[]{:S(2)}) collective-permute-start(bf16[8,32,128]{2,1,0:T(8,128)(2,1)S(1)} %bitcast.25), channel_id=1, source_target_pairs={{0,8},{16,24},{8,0},{24,16},{1,9},{17,25},{9,1},{25,17},{2,10},{18... | collective-permute-start | bytes 196616 | tf_op jit(solution)/shard_map/ppermute | solution.py:264
  7.6 8.6 %copy-start.4 = (bf16[3,3,3,64,8]{3,4,2,1,0:T(8,128)(2,1)S(1)}, bf16[3,3,3,64,8]{3,4,2,1,0:T(8,128)(2,1)}, u32[]{:S(2)}) copy-start(bf16[3,3,3,64,8]{3,4,2,1,0:T(8,128)(2,1)} %param.17) | copy-start | bytes 82948
  7.6 8.6 %copy-start.5 = (f32[64,64]{1,0:T(8,128)S(1)}, f32[64,64]{1,0:T(8,128)}, u32[]{:S(2)}) copy-start(f32[64,64]{1,0:T(8,128)} %tw_ref.1) | copy-start | bytes 49156
  7.7 8.6 %copy-start.6 = (f32[1000,2]{0,1:T(2,128)S(1)}, f32[1000,2]{0,1:T(2,128)}, u32[]{:S(2)}) copy-start(f32[1000,2]{0,1:T(2,128)} %param.12) | copy-start | bytes 24004
  7.8 8.5 %copy-start.1 = (bf16[3,3,3,64,64]{4,3,2,1,0:T(8,128)(2,1)S(1)}, bf16[3,3,3,64,64]{4,3,2,1,0:T(8,128)(2,1)}, u32[]{:S(2)}) copy-start(bf16[3,3,3,64,64]{4,3,2,1,0:T(8,128)(2,1)} %wa_ref.1) | copy-start | bytes 663556
  7.8 8.5 %copy-start.2 = (bf16[3,3,3,64,64]{4,3,2,1,0:T(8,128)(2,1)S(1)}, bf16[3,3,3,64,64]{4,3,2,1,0:T(8,128)(2,1)}, u32[]{:S(2)}) copy-start(bf16[3,3,3,64,64]{4,3,2,1,0:T(8,128)(2,1)} %wb_ref.1) | copy-start | bytes 663556
  10.6 5.7 %copy-start.3 = (bf16[3,3,3,8,64]{4,3,2,1,0:T(8,128)(2,1)S(1)}, bf16[3,3,3,8,64]{4,3,2,1,0:T(8,128)(2,1)}, u32[]{:S(2)}) copy-start(bf16[3,3,3,8,64]{4,3,2,1,0:T(8,128)(2,1)} %wi_ref.1) | copy-start | bytes 82948
  10.6 6.4 %collective-permute-start.3 = (bf16[4,96,128]{2,1,0:T(8,128)(2,1)S(1)}, bf16[4,96,128]{2,1,0:T(8,128)(2,1)S(1)}, u32[]{:S(2)}, u32[]{:S(2)}) collective-permute-start(bf16[4,96,128]{2,1,0:T(8,128)(2,1)S(1)} %get-tuple-element.17), channel_id=1, source_target_pairs={{1,2},{3,4},{5,6},{2,1},{4,3},{6,5},{9,10},{11,12},{13,14},{10,9},... | collective-permute-start | bytes 294920 | tf_op jit(solution)/shard_map/ppermute | solution.py:264
  12.6 4.5 %collective-permute-start.2 = (bf16[4,96,128]{2,1,0:T(8,128)(2,1)S(1)}, bf16[4,96,128]{2,1,0:T(8,128)(2,1)S(1)}, u32[]{:S(2)}, u32[]{:S(2)}) collective-permute-start(bf16[4,96,128]{2,1,0:T(8,128)(2,1)S(1)} %get-tuple-element.18), channel_id=1, source_target_pairs={{0,1},{2,3},{4,5},{6,7},{1,0},{3,2},{5,4},{7,6},{8,9},{10,11},{12,... | collective-permute-start | bytes 294920 | tf_op jit(solution)/shard_map/ppermute | solution.py:264
  16.3 0.9 %copy-start = (f32[1,8,4,8,128]{4,3,2,1,0:T(8,128)S(1)}, f32[1,8,4,8,128]{4,3,2,1,0:T(8,128)}, u32[]{:S(2)}) copy-start(f32[1,8,4,8,128]{4,3,2,1,0:T(8,128)} %param.9) | copy-start | bytes 393220
  36.3 0.7 %collective-permute-start.4 = (f32[64,128]{1,0:T(8,128)S(1)}, f32[64,128]{1,0:T(8,128)S(1)}, u32[]{:S(2)}, u32[]{:S(2)}) collective-permute-start(f32[64,128]{1,0:T(8,128)S(1)} %slice_bitcast_fusion), channel_id=1, source_target_pairs={{0,128},{32,160},{64,192},{96,224},{1,129},{33,161},{65,193},{97,2... | collective-permute-start | bytes 98312 | tf_op jit(solution)/shard_map/ppermute | solution.py:214
  37.0 16.7 %collective-permute-start.6 = (f32[64,128]{1,0:T(8,128)S(1)}, f32[64,128]{1,0:T(8,128)S(1)}, u32[]{:S(2)}, u32[]{:S(2)}) collective-permute-start(f32[64,128]{1,0:T(8,128)S(1)} %fusion.2), channel_id=1, source_target_pairs={{128,384},{160,416},{192,448},{224,480},{129,385},{161,417},{193,4... | collective-permute-start | bytes 98312 | tf_op jit(solution)/shard_map/ppermute | solution.py:216
  38.3 15.4 %collective-permute-start.5 = (f32[64,128]{1,0:T(8,128)S(1)}, f32[64,128]{1,0:T(8,128)S(1)}, u32[]{:S(2)}, u32[]{:S(2)}) collective-permute-start(f32[64,128]{1,0:T(8,128)S(1)} %fusion.2), channel_id=1, source_target_pairs={{128,256},{160,288},{192,320},{224,352},{256,384},{288,416},{320,4... | collective-permute-start | bytes 98312 | tf_op jit(solution)/shard_map/ppermute | solution.py:217

commit v4 on v3

--- a/solution.py
+++ b/solution.py
@@ -1,11 +1,10 @@
-import functools
-
 import jax
 import jax.numpy as jnp
 from jax import lax
 from jax.experimental import pallas as pl
 from jax.experimental.pallas import tpu as pltpu
 from jax.sharding import PartitionSpec as P
+
 
 F32 = jnp.float32
 BF16 = jnp.bfloat16
@@ -52,7 +51,8 @@
 
 
 def silu(x):
-    return x / (1.0 + jnp.exp(-x))
+    half = 0.5 * x
+    return half + half * jnp.tanh(half)
 
 
 def shifted(h):
@@ -212,10 +212,11 @@
     sums = local(scan_kernel, pieces.shape, pieces)
     total = sums[team - 1]
     first = lax.ppermute(total, axis, to(0, 1))
+    wrap = lax.ppermute(total, axis, to(0, 3))
+    far = lax.ppermute(total, axis, to(1, 3))
     half = total + first
-    far = lax.ppermute(half, axis, to(1, 3))
     near = lax.ppermute(half, axis, to(1, 2) + to(2, 3))
-    return swap(local(add_kernel, sums.shape, sums, first, near, far)).reshape(shape)
+    return swap(local(add_kernel, sums.shape, sums, first, wrap, far, near)).reshape(shape)
 
 
 def vmem():
@@ -257,12 +258,12 @@
 
 def exchange(up, down, axis):
     size = lax.axis_size(axis)
-    got = []
-    for start in (0, 1):
+    got = {}
+    for start in (1, 0):
         pairs = [(i, i + 1) for i in range(start, size - 1, 2)]
         send = up if up is down else jnp.where(is_odd(axis) == (start == 1), up, down)
-        got.append(lax.ppermute(send, axis, pairs + [(j, i) for i, j in pairs]))
-    return got
+        got[start] = lax.ppermute(send, axis, pairs + [(j, i) for i, j in pairs])
+    return got[0], got[1]
 
 
 def on_device(state, step_index, sched_index, coef_table, time_weight, w_in, w_mid1, w_mid2, w_out):

time: 64 us -> 62.5 us (0.977)
  the two profiles are of different devices: /device:TPU:426 before, /device:TPU:10 now
where the time goes in v4:
time: 62.5 us; the launch traced here: 62.1 us
  starting transfers between devices  23.5 us (38%)
  blocking collectives  20.3 us (32%)
  Pallas kernels  10.4 us (17%)
  waiting for transfers between devices  4.23 us (7%)
  between operations  1.58 us (3%)
  other arithmetic  1.11 us (2%)
  local copies, waits for them, and re-layouts  0.88 us (1%)
    all_to_all x2, blocking collectives, swap(): return lax.all_to_all(v, axis, 0, 0, axis_index_groups=teams, tiled=True)  20.3 us
    ppermute x4, starting transfers between devices, exchange(): got[start] = lax.ppermute(send, axis, pairs + [(j, i) for i, j in pairs])  10.8 us
    pallas_call x1, Pallas kernels, net_call(): pl.pallas_call(net_kernel, out_shape=pltpu.VMEM(own.shape, F32), in_specs...  9.67 us
    ppermute x1, starting transfers between devices, entering(): first = lax.ppermute(total, axis, to(0, 1))  9.09 us
    ppermute x4, waiting for transfers between devices, exchange(): got[start] = lax.ppermute(send, axis, pairs + [(j, i) for i, j in pairs])  2.78 us
    ppermute x1, starting transfers between devices, entering(): wrap = lax.ppermute(total, axis, to(0, 3))  2.24 us
    ppermute x1, waiting for transfers between devices, entering(): wrap = lax.ppermute(total, axis, to(0, 3))  1.44 us
  transfers between devices with their start and end apart: 8, of which 2 were waited for; matrix products, arithmetic and copies ran while one was open for 0% of the time, Pallas kernels for 1%

profile of v4, /device:TPU:10, one launch (start us, length us, event | category | flops | bytes accessed | tf_op | source)
XLA Modules:
  0.0 62.1 jit_solution(5216579356379677221)
XLA Ops:
  0.0 0.9 %convert_bitcast_fusion = bf16[8,4,8,128]{3,0,1,2:T(8,128)(2,1)S(1)} fusion(f32[1,8,4,8,128]{4,3,2,1,0:T(8,128)} %param.9), kind=kLoop, calls=%fused_computation.5 | loop fusion | flops 32768 | bytes 196608 | tf_op jit(solution)/shard_map/transpose | solution.py:274
  1.0 3.4 %collective-permute-start.1 = (bf16[8,32,128]{2,1,0:T(8,128)(2,1)S(1)}, bf16[8,32,128]{2,1,0:T(8,128)(2,1)S(1)}, u32[]{:S(2)}, u32[]{:S(2)}) collective-permute-start(bf16[8,32,128]{2,1,0:T(8,128)(2,1)S(1)} %bitcast.24), channel_id=1, source_target_pairs={{8,16},{16,8},{9,17},{17,9},{10,18},{18,10},{11,19},{19,11},{12,20... | collective-permute-start | bytes 196616 | tf_op jit(solution)/shard_map/ppermute | solution.py:265
  4.4 1.9 %collective-permute-start = (bf16[8,32,128]{2,1,0:T(8,128)(2,1)S(1)}, bf16[8,32,128]{2,1,0:T(8,128)(2,1)S(1)}, u32[]{:S(2)}, u32[]{:S(2)}) collective-permute-start(bf16[8,32,128]{2,1,0:T(8,128)(2,1)S(1)} %bitcast.25), channel_id=1, source_target_pairs={{0,8},{16,24},{8,0},{24,16},{1,9},{17,25},{9,1},{25,17},{2,10},{18... | collective-permute-start | bytes 196616 | tf_op jit(solution)/shard_map/ppermute | solution.py:265
  7.6 0.0 copy-start.4
  7.6 0.0 copy-start.5
  7.7 0.0 copy-start.6
  7.7 0.1 fusion
  7.8 0.0 copy-start.1
  7.8 0.0 copy-start.2
  7.8 0.0 collective-permute-done.1.za_ref
  7.8 2.7 %collective-permute-done.zb_ref = bf16[8,32,128]{2,1,0:T(8,128)(2,1)S(1)} collective-permute-done((bf16[8,32,128]{2,1,0:T(8,128)(2,1)S(1)}, bf16[8,32,128]{2,1,0:T(8,128)(2,1)S(1)}, u32[]{:S(2)}, u32[]{:S(2)}) %collective-permute-start) | collective-permute-done | bytes 65568 | tf_op jit(solution)/shard_map/ppermute | solution.py:265
  10.6 0.0 copy-start.3
  10.6 1.9 %collective-permute-start.3 = (bf16[4,96,128]{2,1,0:T(8,128)(2,1)S(1)}, bf16[4,96,128]{2,1,0:T(8,128)(2,1)S(1)}, u32[]{:S(2)}, u32[]{:S(2)}) collective-permute-start(bf16[4,96,128]{2,1,0:T(8,128)(2,1)S(1)} %get-tuple-element.17), channel_id=1, source_target_pairs={{1,2},{3,4},{5,6},{2,1},{4,3},{6,5},{9,10},{11,12},{13,14},{10,9},... | collective-permute-start | bytes 294920 | tf_op jit(solution)/shard_map/ppermute | solution.py:265
  12.6 3.6 %collective-permute-start.2 = (bf16[4,96,128]{2,1,0:T(8,128)(2,1)S(1)}, bf16[4,96,128]{2,1,0:T(8,128)(2,1)S(1)}, u32[]{:S(2)}, u32[]{:S(2)}) collective-permute-start(bf16[4,96,128]{2,1,0:T(8,128)(2,1)S(1)} %get-tuple-element.18), channel_id=1, source_target_pairs={{0,1},{2,3},{4,5},{6,7},{1,0},{3,2},{5,4},{7,6},{8,9},{10,11},{12,... | collective-permute-start | bytes 294920 | tf_op jit(solution)/shard_map/ppermute | solution.py:265
  16.1 0.1 maximum_bitcast_fusion.feats_ref
  16.3 0.0 copy-start
  16.3 0.7 %prep.1 = (f32[2,8,128]{2,1,0:T(8,128)S(1)}, f32[64,128]{1,0:T(8,128)S(1)}, bf16[128,288]{1,0:T(8,128)(2,1)S(1)}, bf16[128,2304]{1,0:T(8,128)(2,1)S(1)}, bf16[12...) custom-call(s32[1]{0:T(128)S(6)} %copy.19.sched, f32[2,1000]{1,0:T(2,128)S(1)} %bitcast.28, ...), custom_call_target="tpu_custom_call" | custom-call | tf_op jit(solution)/shard_map/prep/pallas_call | solution.py:294
  17.0 0.0 collective-permute-done.3.ya_ref
  17.0 0.0 collective-permute-done.2.yb_ref
  17.1 0.1 copy-done
  17.2 9.7 %net.1 = f32[8,4,8,128]{3,2,1,0:T(8,128)S(1)} custom-call(f32[2,8,128]{2,1,0:T(8,128)S(1)} %get-tuple-element.11.coef, bf16[8,32,128]{2,1,0:T(8,128)(2,1)S(1)} %bitcast.26, bf16[8,32,128]{2,1,0:T(8,128)(2,1)S(1)} %collective-permute-done.zb_ref, bf16[8,32,128]{2,1,0:T(8,128)(2,1)S(1)} %collective-permute-done.1.za_ref, ...), custom_call_target="tpu_custom_call" | custom-call | tf_op jit(solution)/shard_map/net/pallas_call | solution.py:233
  26.8 12.0 %all_to_all.10.d_ref = f32[4,64,128]{2,1,0:T(8,128)S(1)} all-to-all(f32[4,64,128]{2,1,0:T(8,128)S(1)} %bitcast.23), channel_id=1, replica_groups={{0,32,64,96},{128,160,192,224},{256,288,320,352},{384,416,448,480},{1,3..., dimensions={0} | all-to-all | bytes 262144 | tf_op jit(solution)/shard_map/all_to_all | solution.py:201
  38.9 9.1 %collective-permute-start.4 = (f32[64,128]{1,0:T(8,128)S(1)}, f32[64,128]{1,0:T(8,128)S(1)}, u32[]{:S(2)}, u32[]{:S(2)}) collective-permute-start(f32[64,128]{1,0:T(8,128)S(1)} %slice_bitcast_fusion), channel_id=1, source_target_pairs={{0,128},{32,160},{64,192},{96,224},{1,129},{33,161},{65,193},{97,2... | collective-permute-start | bytes 98312 | tf_op jit(solution)/shard_map/ppermute | solution.py:214
  48.0 0.7 %collective-permute-start.6 = (f32[64,128]{1,0:T(8,128)S(1)}, f32[64,128]{1,0:T(8,128)S(1)}, u32[]{:S(2)}, u32[]{:S(2)}) collective-permute-start(f32[64,128]{1,0:T(8,128)S(1)} %slice_bitcast_fusion), channel_id=1, source_target_pairs={{128,384},{160,416},{192,448},{224,480},{129,385},{161,417},{193,4... | collective-permute-start | bytes 98312 | tf_op jit(solution)/shard_map/ppermute | solution.py:216
  48.7 2.2 %collective-permute-start.5 = (f32[64,128]{1,0:T(8,128)S(1)}, f32[64,128]{1,0:T(8,128)S(1)}, u32[]{:S(2)}, u32[]{:S(2)}) collective-permute-start(f32[64,128]{1,0:T(8,128)S(1)} %slice_bitcast_fusion), channel_id=1, source_target_pairs={{0,384},{32,416},{64,448},{96,480},{1,385},{33,417},{65,449},{97,4... | collective-permute-start | bytes 98312 | tf_op jit(solution)/shard_map/ppermute | solution.py:215
  50.9 0.0 collective-permute-done.4.refs_0_
  50.9 0.7 %collective-permute-start.7 = (f32[64,128]{1,0:T(8,128)S(1)}, f32[64,128]{1,0:T(8,128)S(1)}, u32[]{:S(2)}, u32[]{:S(2)}) collective-permute-start(f32[64,128]{1,0:T(8,128)S(1)} %fusion.2), channel_id=1, source_target_pairs={{128,256},{160,288},{192,320},{224,352},{256,384},{288,416},{320,4... | collective-permute-start | bytes 98312 | tf_op jit(solution)/shard_map/ppermute | solution.py:218
  51.6 0.0 collective-permute-done.6.refs_2_
  51.6 1.4 %collective-permute-done.5.refs_1_ = f32[64,128]{1,0:T(8,128)S(1)} collective-permute-done((f32[64,128]{1,0:T(8,128)S(1)}, f32[64,128]{1,0:T(8,128)S(1)}, u32[]{:S(2)}, u32[]{:S(2)}) %collective-permute-start.5) | collective-permute-done | bytes 32800 | tf_op jit(solution)/shard_map/ppermute | solution.py:215
  53.1 0.0 collective-permute-done.7.refs_3_
  53.1 8.3 %all_to_all.11 = f32[4,64,128]{2,1,0:T(8,128)S(1)} all-to-all(f32[4,64,128]{2,1,0:T(8,128)S(1)} %shard_map.92), channel_id=1, replica_groups={{0,32,64,96},{128,160,192,224},{256,288,320,352},{384,416,448,480},{1,3..., dimensions={0} | all-to-all | bytes 262144 | tf_op jit(solution)/shard_map/all_to_all | solution.py:201
  61.4 0.7 %copy.20 = f32[1,8,4,8,128]{4,3,2,1,0:T(8,128)} copy(f32[1,8,4,8,128]{4,3,2,1,0:T(8,128)S(1)} %bitcast.29) | data formatting | bytes 262144
  (16 shorter events, 0.2 us)
Async XLA Ops:
  1.0 6.8 %collective-permute-start.1 = (bf16[8,32,128]{2,1,0:T(8,128)(2,1)S(1)}, bf16[8,32,128]{2,1,0:T(8,128)(2,1)S(1)}, u32[]{:S(2)}, u32[]{:S(2)}) collective-permute-start(bf16[8,32,128]{2,1,0:T(8,128)(2,1)S(1)} %bitcast.24), channel_id=1, source_target_pairs={{8,16},{16,8},{9,17},{17,9},{10,18},{18,10},{11,19},{19,11},{12,20... | collective-permute-start | bytes 196616 | tf_op jit(solution)/shard_map/ppermute | solution.py:265
  4.4 6.2 %collective-permute-start = (bf16[8,32,128]{2,1,0:T(8,128)(2,1)S(1)}, bf16[8,32,128]{2,1,0:T(8,128)(2,1)S(1)}, u32[]{:S(2)}, u32[]{:S(2)}) collective-permute-start(bf16[8,32,128]{2,1,0:T(8,128)(2,1)S(1)} %bitcast.25), channel_id=1, source_target_pairs={{0,8},{16,24},{8,0},{24,16},{1,9},{17,25},{9,1},{25,17},{2,10},{18... | collective-permute-start | bytes 196616 | tf_op jit(solution)/shard_map/ppermute | solution.py:265
  7.6 8.6 %copy-start.4 = (bf16[3,3,3,64,8]{3,4,2,1,0:T(8,128)(2,1)S(1)}, bf16[3,3,3,64,8]{3,4,2,1,0:T(8,128)(2,1)}, u32[]{:S(2)}) copy-start(bf16[3,3,3,64,8]{3,4,2,1,0:T(8,128)(2,1)} %param.17) | copy-start | bytes 82948
  7.6 8.6 %copy-start.5 = (f32[64,64]{1,0:T(8,128)S(1)}, f32[64,64]{1,0:T(8,128)}, u32[]{:S(2)}) copy-start(f32[64,64]{1,0:T(8,128)} %tw_ref.1) | copy-start | bytes 49156
  7.7 8.6 %copy-start.6 = (f32[1000,2]{0,1:T(2,128)S(1)}, f32[1000,2]{0,1:T(2,128)}, u32[]{:S(2)}) copy-start(f32[1000,2]{0,1:T(2,128)} %param.12) | copy-start | bytes 24004
  7.8 8.5 %copy-start.1 = (bf16[3,3,3,64,64]{4,3,2,1,0:T(8,128)(2,1)S(1)}, bf16[3,3,3,64,64]{4,3,2,1,0:T(8,128)(2,1)}, u32[]{:S(2)}) copy-start(bf16[3,3,3,64,64]{4,3,2,1,0:T(8,128)(2,1)} %wa_ref.1) | copy-start | bytes 663556
  7.8 8.5 %copy-start.2 = (bf16[3,3,3,64,64]{4,3,2,1,0:T(8,128)(2,1)S(1)}, bf16[3,3,3,64,64]{4,3,2,1,0:T(8,128)(2,1)}, u32[]{:S(2)}) copy-start(bf16[3,3,3,64,64]{4,3,2,1,0:T(8,128)(2,1)} %wb_ref.1) | copy-start | bytes 663556
  10.6 5.7 %copy-start.3 = (bf16[3,3,3,8,64]{4,3,2,1,0:T(8,128)(2,1)S(1)}, bf16[3,3,3,8,64]{4,3,2,1,0:T(8,128)(2,1)}, u32[]{:S(2)}) copy-start(bf16[3,3,3,8,64]{4,3,2,1,0:T(8,128)(2,1)} %wi_ref.1) | copy-start | bytes 82948
  10.6 6.4 %collective-permute-start.3 = (bf16[4,96,128]{2,1,0:T(8,128)(2,1)S(1)}, bf16[4,96,128]{2,1,0:T(8,128)(2,1)S(1)}, u32[]{:S(2)}, u32[]{:S(2)}) collective-permute-start(bf16[4,96,128]{2,1,0:T(8,128)(2,1)S(1)} %get-tuple-element.17), channel_id=1, source_target_pairs={{1,2},{3,4},{5,6},{2,1},{4,3},{6,5},{9,10},{11,12},{13,14},{10,9},... | collective-permute-start | bytes 294920 | tf_op jit(solution)/shard_map/ppermute | solution.py:265
  12.6 4.5 %collective-permute-start.2 = (bf16[4,96,128]{2,1,0:T(8,128)(2,1)S(1)}, bf16[4,96,128]{2,1,0:T(8,128)(2,1)S(1)}, u32[]{:S(2)}, u32[]{:S(2)}) collective-permute-start(bf16[4,96,128]{2,1,0:T(8,128)(2,1)S(1)} %get-tuple-element.18), channel_id=1, source_target_pairs={{0,1},{2,3},{4,5},{6,7},{1,0},{3,2},{5,4},{7,6},{8,9},{10,11},{12,... | collective-permute-start | bytes 294920 | tf_op jit(solution)/shard_map/ppermute | solution.py:265
  16.3 0.9 %copy-start = (f32[1,8,4,8,128]{4,3,2,1,0:T(8,128)S(1)}, f32[1,8,4,8,128]{4,3,2,1,0:T(8,128)}, u32[]{:S(2)}) copy-start(f32[1,8,4,8,128]{4,3,2,1,0:T(8,128)} %param.9) | copy-start | bytes 393220
  38.9 12.0 %collective-permute-start.4 = (f32[64,128]{1,0:T(8,128)S(1)}, f32[64,128]{1,0:T(8,128)S(1)}, u32[]{:S(2)}, u32[]{:S(2)}) collective-permute-start(f32[64,128]{1,0:T(8,128)S(1)} %slice_bitcast_fusion), channel_id=1, source_target_pairs={{0,128},{32,160},{64,192},{96,224},{1,129},{33,161},{65,193},{97,2... | collective-permute-start | bytes 98312 | tf_op jit(solution)/shard_map/ppermute | solution.py:214
  48.0 3.6 %collective-permute-start.6 = (f32[64,128]{1,0:T(8,128)S(1)}, f32[64,128]{1,0:T(8,128)S(1)}, u32[]{:S(2)}, u32[]{:S(2)}) collective-permute-start(f32[64,128]{1,0:T(8,128)S(1)} %slice_bitcast_fusion), channel_id=1, source_target_pairs={{128,384},{160,416},{192,448},{224,480},{129,385},{161,417},{193,4... | collective-permute-start | bytes 98312 | tf_op jit(solution)/shard_map/ppermute | solution.py:216
  48.7 4.4 %collective-permute-start.5 = (f32[64,128]{1,0:T(8,128)S(1)}, f32[64,128]{1,0:T(8,128)S(1)}, u32[]{:S(2)}, u32[]{:S(2)}) collective-permute-start(f32[64,128]{1,0:T(8,128)S(1)} %slice_bitcast_fusion), channel_id=1, source_target_pairs={{0,384},{32,416},{64,448},{96,480},{1,385},{33,417},{65,449},{97,4... | collective-permute-start | bytes 98312 | tf_op jit(solution)/shard_map/ppermute | solution.py:215
  50.9 2.1 %collective-permute-start.7 = (f32[64,128]{1,0:T(8,128)S(1)}, f32[64,128]{1,0:T(8,128)S(1)}, u32[]{:S(2)}, u32[]{:S(2)}) collective-permute-start(f32[64,128]{1,0:T(8,128)S(1)} %fusion.2), channel_id=1, source_target_pairs={{128,256},{160,288},{192,320},{224,352},{256,384},{288,416},{320,4... | collective-permute-start | bytes 98312 | tf_op jit(solution)/shard_map/ppermute | solution.py:218
